TPU v7x, 32 devices: a whole 2x2x4 slice. The times are simulated.
32 devices in a mesh: rep: 2 (over y), shard: 16 (over z, x, core).
Axes of the slice: x: 2, y: 2, z: 4, core: 2. Of those that a mesh axis runs over, the one named last changes fastest.
Arguments:
- tokens: bfloat16 [16384, 1024], P(('rep', 'shard')), may hold values from -6 to 6
- cotangent: bfloat16 [16384, 1024], P(('rep', 'shard')), may hold values from -6 to 6
- send_slot: int32 [16384], P(('rep', 'shard')), may hold values from 0 to 1023, as said below
- recv_slot: int32 [16384], P(('rep', 'shard')), may hold values from 0 to 1023, as said below
- lengths: int32 [32, 4], P(('rep', 'shard')), may hold values from 1 to 384, 512 in all within a row
- variate: int32 [16384], P(('rep', 'shard')), may hold values from 0 to 3
- valid_mask: int32 [16384], P(('rep', 'shard')), may hold values from 0 to 1, as said below
- norm_attn: bfloat16 [1024], P('shard'), may hold values from 0.5 to 1.5
- w_query: bfloat16 [1024, 1024], P('shard'), may hold values from -0.1875 to 0.1875
- w_key: bfloat16 [1024, 1024], P('shard'), may hold values from -0.1875 to 0.1875
- w_value: bfloat16 [1024, 1024], P('shard'), may hold values from -0.1875 to 0.1875
- w_out: bfloat16 [1024, 1024], P('shard'), may hold values from -0.75 to 0.75
- variate_bias: float32 [2, 16], replicated, may hold values from -3 to 3
- norm_mlp: bfloat16 [1024], P('shard'), may hold values from 0.5 to 1.5
- w_gate: bfloat16 [1024, 4096], P('shard'), may hold values from -0.1875 to 0.1875
- w_up: bfloat16 [1024, 4096], P('shard'), may hold values from -0.1875 to 0.1875
- w_down: bfloat16 [4096, 1024], P('shard'), may hold values from -0.1875 to 0.1875
Outputs:
- output: bfloat16 [16384, 1024], P(('rep', 'shard'))
- input_grad: bfloat16 [16384, 1024], P(('rep', 'shard'))
- grad_norm_attn: float32 [1024], P('shard')
- grad_query: float32 [1024, 1024], P('shard')
- grad_key: float32 [1024, 1024], P('shard')
- grad_value: float32 [1024, 1024], P('shard')
- grad_out: float32 [1024, 1024], P('shard')
- grad_bias: float32 [2, 16], replicated
- grad_norm_mlp: float32 [1024], P('shard')
- grad_gate: float32 [1024, 4096], P('shard')
- grad_up: float32 [1024, 4096], P('shard')
- grad_down: float32 [4096, 1024], P('shard')
- root_means: float32 [5], replicated
Inputs may be any that keep to these rules, and one draw needn't show every extreme that they name: send_slot[i] = (index in the rep group of the device that gets token i) * 64 + the token's rank among its device's tokens going there. The values on one device are distinct; a device sends to each device of its group a multiple of 16 tokens and at most 64, and some device sends exactly 64 to the last device of its group. recv_slot[t] = (index in the group of the sending device) * 64 + the token's rank there; the values on one device are distinct. With send_slot it describes one permutation of the tokens of each rep group, every device receives exactly 512 tokens, and the last device of some group sends exactly 64 to some device. `valid_mask`: the first row of every device's block is 1.
All inputs are finite; a program needn't handle non-finite values.
Results may differ from a plain program's by a relative error of at most 0.017.
Values may be sent and summed in bfloat16 or wider, within the bound.
A program may use at most 256 MiB of HBM per device.

v0:
```python
import functools
import math

import jax
import jax.numpy as jnp
from jax import lax
from jax.experimental import pallas as pl
from jax.experimental.pallas import tpu as pltpu
from jax.sharding import PartitionSpec as P

MESH = pl.DeviceIdType.MESH
DMA = pltpu.SemaphoreType.DMA
epsilon = 1e-06
masked_score = -1e30
VMEM_LIMIT = 62 << 20


def angle_tables(position, head_dim):
    half_dim = head_dim // 2
    inverse_freq = 1.0 / 10000.0 ** (jnp.arange(half_dim, dtype=jnp.float32) / half_dim)
    theta_angle = position.astype(jnp.float32)[:, None] * inverse_freq[None, :]
    return (jnp.cos(theta_angle), jnp.sin(theta_angle))


def layout(lengths_row, tok_rows):
    slot_ids = jnp.arange(tok_rows, dtype=jnp.int32)
    seq_ends = jnp.cumsum(lengths_row)
    segment = jnp.sum((slot_ids[:, None] >= seq_ends[None, :]).astype(jnp.int32), axis=1)
    starts = seq_ends - lengths_row
    chosen = segment[:, None] == jnp.arange(lengths_row.shape[0], dtype=jnp.int32)[None, :]
    begins = jnp.sum(jnp.where(chosen, starts[None, :], 0), axis=1)
    return (segment, slot_ids - begins)


def ring_place(chip, chips):
    return jnp.where(chip % 2 == 0, chip // 2, chips - 1 - chip // 2)


def ring_chip(place, chips):
    wrapped = lax.rem(place + 2 * chips, chips)
    return jnp.where(wrapped < chips // 2, 2 * wrapped, 2 * (chips - 1 - wrapped) + 1)


class Spot:
    def __init__(self, shards):
        self.shards = shards
        self.chips = shards // 2
        self.half = self.chips // 2
        self.rep = lax.axis_index("rep")
        self.shard = lax.axis_index("shard")
        self.core = lax.rem(self.shard, 2)
        self.place = ring_place(self.shard // 2, self.chips)
        self.sibling = self.shard + 1 - 2 * self.core

    def block(self, place, core=None):
        return 2 * ring_chip(place, self.chips) + (self.core if core is None else core)

    def along(self, way, distance):
        return self.place - distance if way == 0 else self.place + distance

    def ahead(self, way):
        return (self.rep, self.block(self.along(way, -1)))


def greet(spot):
    barrier = pltpu.get_barrier_semaphore()

    def peer(k, carry):
        target = lax.rem(spot.shard + k, spot.shards)
        pl.semaphore_signal(barrier, inc=1, device_id=(spot.rep, target), device_id_type=MESH)
        return carry

    lax.fori_loop(1, spot.shards, peer, 0)
    pl.semaphore_signal(
        barrier, inc=1, device_id=(1 - spot.rep, spot.shard), device_id_type=MESH
    )
    pl.semaphore_wait(barrier, spot.shards)


def remote(src, dst, sems, at, target):
    return pltpu.make_async_remote_copy(
        src_ref=src,
        dst_ref=dst,
        send_sem=sems[0].at[at],
        recv_sem=sems[1].at[at],
        device_id=target,
        device_id_type=MESH,
    )


class Swap:
    def __init__(self, spot, source, arrived, sems, own_sem):
        self.spot, self.sems = spot, sems
        self.source, self.arrived = source, arrived
        self.capacity = arrived.shape[0] // spot.shards
        self.own = pltpu.make_async_copy(
            self.part(spot.shard), arrived.at[self.rows(spot.shard)], own_sem
        )

    def rows(self, shard):
        return pl.ds(pl.multiple_of(shard * self.capacity, 8), self.capacity)

    def part(self, shard):
        if self.source.shape[0] == self.capacity:
            return self.source
        return self.source.at[self.rows(shard)]

    def copy(self, k):
        spot = self.spot
        target = lax.rem(spot.shard + 7 * k, spot.shards)
        return remote(
            self.part(target),
            self.arrived.at[self.rows(spot.shard)],
            self.sems,
            (k,),
            (spot.rep, target),
        )

    def start(self, slot, slots):
        size = -(-self.spot.shards // slots)

        def one(k, carry):
            @pl.when(k == 0)
            def _():
                self.own.start()

            @pl.when(k > 0)
            def _():
                self.copy(k).start()

            return carry

        first = jnp.minimum(slot * size, self.spot.shards)
        lax.fori_loop(first, jnp.minimum(first + size, self.spot.shards), one, 0)

    def finish(self):
        def one(k, carry):
            self.copy(k).wait()
            return carry

        lax.fori_loop(1, self.spot.shards, one, 0)
        self.own.wait()


class Gather:
    def __init__(self, spot, lent, shard_ref, full_ref, sems):
        self.spot, self.lent, self.shard_ref, self.full_ref = spot, lent, shard_ref, full_ref
        self.rows = shard_ref.shape[0]
        self.unit = shard_ref.shape[1] // 8
        self.kept = 8 - lent
        self.ring_sems, self.near_sems, self.far_sems, self.far_near_sems = (
            sems[0:2],
            sems[2:4],
            sems[4:6],
            sems[6:8],
        )
        self.whole_sems, self.own_sem = sems[8:10], sems[10]

    def span(self, way, short):
        first, count = self.lent * self.spot.rep, self.kept
        if short:
            first, count = first + way * (count // 2), count // 2
        return pl.ds(pl.multiple_of(first * self.unit, 128), count * self.unit)

    def region(self, way, hop, short):
        block = self.spot.block(self.spot.along(way, hop))
        return self.full_ref.at[pl.ds(block * self.rows, self.rows), self.span(way, short)]

    def ring(self, way, hop, short, source=None):
        region = self.region(way, hop, short)
        return remote(
            region if source is None else source,
            region,
            self.ring_sems,
            (way, hop),
            self.spot.ahead(way),
        )

    def near(self, way, hop, short):
        region = self.region(way, hop + 1, short)
        target = (self.spot.rep, self.spot.sibling)
        return remote(region, region, self.near_sems, (way, hop), target)

    def lent_region(self, way, hop, owner):
        block = self.spot.block(self.spot.along(way, hop + 1))
        columns = pl.ds(
            pl.multiple_of(self.kept * owner * self.unit, 128), self.lent * self.unit
        )
        return self.full_ref.at[pl.ds(block * self.rows, self.rows), columns]

    def far(self, way, hop):
        region = self.lent_region(way, hop, self.spot.rep)
        target = (1 - self.spot.rep, self.spot.shard)
        return remote(region, region, self.far_sems, (way, hop), target)

    def far_near(self, way, hop):
        region = self.lent_region(way, hop, 1 - self.spot.rep)
        target = (self.spot.rep, self.spot.sibling)
        return remote(region, region, self.far_near_sems, (way, hop), target)

    def own(self):
        spot = self.spot
        mine = self.full_ref.at[pl.ds(spot.shard * self.rows, self.rows)]
        whole = remote(self.shard_ref, mine, self.whole_sems, (0,), (spot.rep, spot.sibling))
        return whole, pltpu.make_async_copy(self.shard_ref, mine, self.own_sem)

    def start(self):
        for way in (0, 1):
            self.ring(way, 0, False, self.shard_ref.at[:, self.span(way, False)]).start()
        for copy in self.own():
            copy.start()

    def step(self, hop):
        final = self.spot.half - 1

        @pl.when(hop < final)
        def _():
            for way in (0, 1):
                self.ring(way, hop, False).wait_recv()

                @pl.when(hop < final - 1)
                def _():
                    self.ring(way, hop + 1, False).start()

                @pl.when(hop == final - 1)
                def _():
                    self.ring(way, hop + 1, True).start()

            for way in (0, 1):
                self.far(way, hop).start()
                self.near(way, hop, False).start()

        @pl.when(hop == final)
        def _():
            for way in (0, 1):
                self.ring(way, hop, True).wait_recv()
            self.far(0, hop).start()
            for way in (0, 1):
                self.near(way, hop, True).start()

        @pl.when(hop > 0)
        def _():
            for way in (0, 1):
                self.relay(way, hop - 1)

    def relay(self, way, hop):
        self.far(way, hop).wait_recv()
        self.far_near(way, hop).start()

    def finish(self):
        final = self.spot.half - 1
        for copy in self.own():
            copy.wait()

        def one(hop, carry):
            for way in (0, 1):
                self.ring(way, hop, False).wait_send()
                self.near(way, hop, False).wait()
                self.far(way, hop).wait_send()
                self.far_near(way, hop).wait()
            return carry

        lax.fori_loop(0, final, one, 0)
        for way in (0, 1):
            self.ring(way, final, True).wait_send()
            self.near(way, final, True).wait()
        self.far(0, final).wait_send()
        self.far_near(0, final).wait()

    @staticmethod
    def scratch(half):
        return [DMA((2, half))] * 8 + [DMA((1,))] * 2 + [DMA]


class GatherAll:
    def __init__(self, spot, lents, swap_count, inputs, outputs, scratch):
        count = len(lents)
        self.spot = spot
        self.gathers = [
            Gather(spot, lents[g], inputs[g], outputs[g], scratch[11 * g : 11 * g + 11])
            for g in range(count)
        ]
        scratch = scratch[11 * count :]
        self.swaps = [
            Swap(
                spot,
                inputs[count + i],
                outputs[count + i],
                scratch[3 * i : 3 * i + 2],
                scratch[3 * i + 2],
            )
            for i in range(swap_count)
        ]

    def start(self):
        greet(self.spot)
        for gather in self.gathers:
            gather.start()

    def exchange(self, slot, slots):
        for swap in self.swaps:
            swap.start(slot, slots)

    def steps(self, slot, slots):
        def one(hop, carry):
            for gather in self.gathers:
                gather.step(hop)
            return carry

        half = self.spot.half
        lax.fori_loop(slot * half // slots, (slot + 1) * half // slots, one, 0)

    def finish_gathers(self):
        for gather in self.gathers:
            gather.relay(0, self.spot.half - 1)
        for gather in self.gathers:
            gather.finish()

    def finish(self):
        self.finish_gathers()
        for swap in self.swaps:
            swap.finish()

    @staticmethod
    def scratch(shards, count, swap_count):
        return Gather.scratch(shards // 4) * count + [
            DMA((shards,)),
            DMA((shards,)),
            DMA,
        ] * swap_count


def gather_kernel(shards, lents, *refs):
    spot = Spot(shards)
    rows_ref, tokens_ref, cotangent_ref = refs[:3]
    count = len(lents)
    pieces, gains_ref, refs = refs[3 : 3 + count], refs[3 + count], refs[4 + count :]
    outputs, packed_out, refs = refs[: count + 2], refs[count + 2], refs[count + 3 :]
    packed_ref, scratch = refs[0], refs[1:]
    work = GatherAll(spot, lents, 2, [*pieces, packed_ref, gains_ref], outputs, scratch)
    work.start()
    chosen = place_rows(rows_ref[0:1, :], packed_ref.shape[0])
    matmul_columns(packed_ref, chosen, tokens_ref)

    def one(hop, carry):
        work.exchange(hop, spot.half)

        @pl.when(hop == 0)
        def _():
            matmul_columns(packed_out, chosen, cotangent_ref)

        work.steps(hop, spot.half)
        return carry

    lax.fori_loop(0, spot.half, one, 0)
    work.finish()


def gather_shapes(shards, pieces, sent, shared):
    return (
        [
            jax.ShapeDtypeStruct((shards * piece.shape[0], piece.shape[1]), piece.dtype)
            for piece in pieces
        ]
        + [jax.ShapeDtypeStruct(rows.shape, rows.dtype) for rows in sent]
        + [
            jax.ShapeDtypeStruct((shards * each.shape[0], each.shape[1]), each.dtype)
            for each in shared
        ]
    )


def gather_call(shards, rows, tokens, cotangent, pieces, lents, gains, collective_id):
    anywhere = pl.BlockSpec(memory_space=pl.ANY)
    inside = pl.BlockSpec(memory_space=pltpu.VMEM)
    count = len(pieces)
    packed = jax.ShapeDtypeStruct((2 * tokens.shape[0], tokens.shape[1]), tokens.dtype)
    results = pl.pallas_call(
        functools.partial(gather_kernel, shards, lents),
        out_shape=[*gather_shapes(shards, pieces, [packed], [gains]), packed],
        in_specs=[inside] * 3 + [anywhere] * (count + 1),
        out_specs=[anywhere] * (count + 2) + [inside],
        scratch_shapes=[
            pltpu.VMEM(packed.shape, packed.dtype),
            *GatherAll.scratch(shards, count, 2),
        ],
        compiler_params=pltpu.CompilerParams(
            collective_id=collective_id, has_side_effects=True, vmem_limit_bytes=VMEM_LIMIT
        ),
    )(rows, tokens, cotangent, *pieces, gains)
    return results[:count], *results[count:]


class Reduce:
    def __init__(self, spot, lent, partial_ref, out_ref, refs, part=0, parts=1):
        self.spot, self.lent, self.partial, self.out = spot, lent, partial_ref, out_ref
        self.block_rows = partial_ref.shape[0] // spot.shards
        self.columns = partial_ref.shape[1]
        self.rows = self.block_rows // parts
        self.offset = part * self.rows
        self.unit = self.columns // 8
        self.kept = 8 - lent
        self.width = self.kept * self.unit
        (
            self.own,
            self.sib,
            self.got,
            self.own_far,
            self.sib_far,
            self.got_far,
            self.got_last,
        ) = refs[:7]
        sems = refs[7:]
        self.load_sem, self.load_far_sem = sems[0], sems[1]
        self.sib_sems, self.sib_far_sems = sems[2:4], sems[4:6]
        self.ring_sems, self.far_sems, self.last_sems = sems[6:8], sems[8:10], sems[10:12]
        self.out_sems = sems[12]

    @staticmethod
    def scratch(shards, lent, rows, columns):
        chips = shards // 2
        unit = columns // 8
        kept, lend = (8 - lent) * unit, lent * unit
        half = jnp.bfloat16
        buffers = [
            pltpu.VMEM((chips, rows, kept), half),
            pltpu.VMEM((chips, rows, kept), half),
            pltpu.VMEM((2, chips // 2, rows, kept), half),
            pltpu.VMEM((chips, rows, lend), half),
            pltpu.VMEM((chips, rows, lend), half),
            pltpu.VMEM((chips, rows, lend), half),
            pltpu.VMEM((rows, kept), half),
        ]
        sems = [DMA((chips,))] * 6 + [DMA((2, chips // 2))] * 2
        sems += [DMA((chips,))] * 2 + [DMA((1,))] * 2 + [DMA((2,))]
        return buffers + sems

    def owner(self, item, core):
        half = self.spot.half
        pair = (item + 1) // 2
        ahead = lax.rem(item, 2) == 1
        distance = half - pair
        place = jnp.where(ahead, self.spot.place + distance, self.spot.place - distance)
        return self.spot.block(place, core)

    def cut(self, item, core, first, count):
        columns = pl.ds(pl.multiple_of(first * self.unit, 128), count * self.unit)
        block = self.owner(item, core)
        first = pl.multiple_of(block * self.block_rows + self.offset, 16)
        return self.partial.at[pl.ds(first, self.rows), columns]

    def kept_cut(self, item, core):
        return self.cut(item, core, self.lent * self.spot.rep, self.kept)

    def lent_cut(self, item, core):
        return self.cut(item, core, self.kept * (1 - self.spot.rep), self.lent)

    def load(self, item):
        source = self.kept_cut(item, self.spot.core)
        return pltpu.make_async_copy(source, self.own.at[item], self.load_sem.at[item])

    def load_far(self, item):
        source = self.lent_cut(item, self.spot.core)
        return pltpu.make_async_copy(source, self.own_far.at[item], self.load_far_sem.at[item])

    def give(self, item):
        source = self.kept_cut(item, 1 - self.spot.core)
        target = (self.spot.rep, self.spot.sibling)
        return remote(source, self.sib.at[item], self.sib_sems, (item,), target)

    def give_far(self, item):
        source = self.lent_cut(item, 1 - self.spot.core)
        target = (self.spot.rep, self.spot.sibling)
        return remote(source, self.sib_far.at[item], self.sib_far_sems, (item,), target)

    def ring(self, way, step, short=False):
        item = 0 if short else 2 * step - 1 + way
        columns = pl.ds(way * self.width // 2, self.width // 2) if short else slice(None)
        return remote(
            self.own.at[item, :, columns],
            self.got.at[way, step, :, columns],
            self.ring_sems,
            (way, step),
            self.spot.ahead(way),
        )

    def far(self, item):
        target = (1 - self.spot.rep, self.spot.shard)
        return remote(
            self.own_far.at[item], self.got_far.at[item], self.far_sems, (item,), target
        )

    @staticmethod
    def out_shape(shards, lent, partial):
        rows, columns = partial.shape[0] // shards, partial.shape[1]
        return jax.ShapeDtypeStruct((2, rows, (8 - lent) * columns // 8), jnp.bfloat16)

    def last(self):
        target = (1 - self.spot.rep, self.spot.shard)
        source = self.own.at[self.spot.chips - 1]
        return remote(source, self.got_last, self.last_sems, (0,), target)

    def start(self, item):
        self.load_far(item).start()
        self.give_far(item).start()
        self.load(item).start()
        self.give(item).start()

    def tiles(self, width, body):
        chunk = width if width <= 768 else 512
        chunks = width // chunk

        def one(i, carry):
            tile, first = i // chunks, lax.rem(i, chunks) * chunk
            body(pl.ds(pl.multiple_of(tile * 16, 16), 16), first, chunk)
            return carry

        lax.fori_loop(0, self.rows // 16 * chunks, one, 0)

    def far_step(self, item):
        self.load_far(item).wait()
        self.give_far(item).wait_recv()

        def add(rows, first, count):
            at = pl.ds(pl.multiple_of(first, 128), count)
            total = self.own_far[item, rows, at].astype(jnp.float32)
            total += self.sib_far[item, rows, at].astype(jnp.float32)
            self.own_far[item, rows, at] = total.astype(jnp.bfloat16)

        self.tiles(self.lent * self.unit, add)
        self.far(item).start()

    def fold(self, item, extra=(), start=0, width=None):
        def add(rows, first, count):
            at = pl.ds(pl.multiple_of(start + first, 128), count)
            total = self.own[item, rows, at].astype(jnp.float32)
            total += self.sib[item, rows, at].astype(jnp.float32)
            for way, step in extra:
                total += self.got[way, step, rows, at].astype(jnp.float32)
            self.own[item, rows, at] = total.astype(jnp.bfloat16)

        self.tiles(self.width if width is None else width, add)

    def ready(self, item):
        self.load(item).wait()
        self.give(item).wait_recv()
        self.far(item).wait_recv()
        offset = self.spot.rep * (self.kept - self.lent) * self.unit

        def add(rows, first, count):
            at = pl.ds(pl.multiple_of(offset + first, 128), count)
            total = self.sib[item, rows, at].astype(jnp.float32)
            lent_at = pl.ds(pl.multiple_of(first, 128), count)
            total += self.got_far[item, rows, lent_at].astype(jnp.float32)
            self.sib[item, rows, at] = total.astype(jnp.bfloat16)

        self.tiles(self.lent * self.unit, add)

    def step(self, step):
        half, chips = self.spot.half, self.spot.chips

        @pl.when(step == 0)
        def _():
            self.ready(0)
            self.fold(0)
            for way in (0, 1):
                self.ring(way, 0, True).start()

        @pl.when((step > 0) & (step < half))
        def _():
            for way in (0, 1):
                item = 2 * step - 1 + way
                self.ready(item)

                @pl.when(step == 1)
                def _():
                    self.ring(way, 0, True).wait_recv()
                    middle = self.width // 2
                    self.fold(item, [(way, 0)], way * middle, middle)
                    self.fold(item, [], (1 - way) * middle, middle)

                @pl.when(step > 1)
                def _():
                    self.ring(way, step - 1).wait_recv()
                    self.fold(item, [(way, step - 1)])

                self.ring(way, step).start()

        @pl.when(step == half)
        def _():
            self.ready(chips - 1)
            for way in (0, 1):
                self.ring(way, half - 1).wait_recv()
            self.fold(chips - 1, [(0, half - 1), (1, half - 1)])
            self.last().start()

        @pl.when(step < half)
        def _():
            self.far_step(2 * step + 1)

            @pl.when(step < half - 1)
            def _():
                self.far_step(2 * step + 2)

    def finish(self):
        spot = self.spot
        rows = pl.ds(self.offset, self.rows)
        mine = pltpu.make_async_copy(
            self.own.at[spot.chips - 1], self.out.at[0, rows], self.out_sems.at[0]
        )
        mine.start()
        self.last().wait()
        theirs = pltpu.make_async_copy(
            self.got_last, self.out.at[1, rows], self.out_sems.at[1]
        )
        theirs.start()
        mine.wait()
        theirs.wait()

        def one(item, carry):
            self.give_far(item).wait_send()
            self.far(item).wait_send()
            self.give(item).wait_send()
            return carry

        lax.fori_loop(0, spot.chips, one, 0)
        for way in (0, 1):
            self.ring(way, 0, True).wait_send()

        def two(step, carry):
            for way in (0, 1):
                self.ring(way, step).wait_send()
            return carry

        lax.fori_loop(1, spot.half, two, 0)


class Tally:
    def __init__(self, spot, mine, out, refs):
        self.spot, self.mine, self.out = spot, mine, out
        self.got, self.half, self.other = refs[0:3]
        self.sems, self.own_sem, self.far_sems = refs[3:5], refs[5], refs[6:8]
        self.own = pltpu.make_async_copy(mine, self.got.at[spot.shard], self.own_sem)

    def copy(self, k):
        spot = self.spot
        target = lax.rem(spot.shard + k, spot.shards)
        return remote(self.mine, self.got.at[spot.shard], self.sems, (k,), (spot.rep, target))

    def far(self):
        target = (1 - self.spot.rep, self.spot.shard)
        return remote(self.half, self.other, self.far_sems, (0,), target)

    def start(self):
        def one(k, carry):
            self.copy(k).start()
            return carry

        lax.fori_loop(1, self.spot.shards, one, 0)
        self.own.start()

    def middle(self):
        def one(k, carry):
            self.copy(k).wait()
            return carry

        lax.fori_loop(1, self.spot.shards, one, 0)
        self.own.wait()

        def add(k, total):
            return total + self.got[k]

        self.half[...] = lax.fori_loop(0, self.spot.shards, add, jnp.zeros_like(self.half))
        self.far().start()

    def finish(self):
        self.far().wait()
        self.out[...] = self.half[...] + self.other[...]

    @staticmethod
    def scratch(shards, shape):
        full = jnp.float32
        return [
            pltpu.VMEM((shards, *shape), full),
            pltpu.VMEM(shape, full),
            pltpu.VMEM(shape, full),
            DMA((shards,)),
            DMA((shards,)),
            DMA,
            DMA((1,)),
            DMA((1,)),
        ]


def matmul(left, right, left_dim=1, right_dim=0):
    return lax.dot_general(
        left, right, (((left_dim,), (right_dim,)), ((), ())), preferred_element_type=jnp.float32
    )


def matmul_columns(out_ref, left, right_ref):
    def one(i, carry):
        at = pl.ds(pl.multiple_of(i * 512, 512), 512)
        part = matmul(left, right_ref[:, at].astype(jnp.bfloat16))
        out_ref[:, at] = part.astype(out_ref.dtype)
        return carry

    lax.fori_loop(0, out_ref.shape[1] // 512, one, 0)


def pick_rows(slot_column, slot_total):
    shape = (slot_column.shape[0], slot_total)
    return (slot_column == lax.broadcasted_iota(jnp.int32, shape, 1)).astype(jnp.bfloat16)


def place_rows(slot_row, slot_total):
    shape = (slot_total, slot_row.shape[1])
    return (slot_row == lax.broadcasted_iota(jnp.int32, shape, 0)).astype(jnp.bfloat16)


def assemble_kernel(rep_ref, *refs):
    raws, plain, refs = refs[:4], refs[4:6], refs[6:]
    plain_outs, outs, whole_ref = refs[:2], refs[2:9], refs[9]
    for source, target in zip(plain, plain_outs, strict=True):
        target[...] = source[...]
    for raw_ref, out_ref in zip(raws, [*outs[:3], whole_ref], strict=True):
        kept = raw_ref.shape[2]
        columns = out_ref.shape[1]
        lent = columns - kept

        def write(low, high, raw_ref=raw_ref, out_ref=out_ref, kept=kept, lent=lent):
            def part(which, first, count):
                return raw_ref[which, :, first : first + count].astype(jnp.float32)

            out_ref[:, 0:lent] = part(low, 0, lent)
            if kept > lent:
                out_ref[:, lent:kept] = part(low, lent, kept - lent) + part(high, 0, kept - lent)
            out_ref[:, kept:] = part(high, kept - lent, lent)

        @pl.when(rep_ref[0, 0] == 0)
        def _(write=write):
            write(0, 1)

        @pl.when(rep_ref[0, 0] != 0)
        def _(write=write):
            write(1, 0)

    width = outs[3].shape[1]
    for i in range(4):
        outs[3 + i][...] = whole_ref[:, i * width : (i + 1) * width]


def local_call(kernel, out_shape, inputs, spaces=None, scratch=()):
    inside = pl.BlockSpec(memory_space=pltpu.VMEM)
    return pl.pallas_call(
        kernel,
        out_shape=out_shape,
        in_specs=spaces or [inside] * len(inputs),
        out_specs=[inside] * len(out_shape),
        scratch_shapes=list(scratch),
        compiler_params=pltpu.CompilerParams(vmem_limit_bytes=VMEM_LIMIT),
    )(*inputs)


def segment_of(index, lengths_ref):
    first = lengths_ref[0, 0]
    second = first + lengths_ref[0, 1]
    third = second + lengths_ref[0, 2]
    return (
        (index >= first).astype(jnp.int32)
        + (index >= second).astype(jnp.int32)
        + (index >= third).astype(jnp.int32)
    )


def pair_masks(columns_ref, rows_ref, lengths_ref, same_ref, hidden_ref):
    size = columns_ref.shape[0]
    shape = (size, size)
    key_id = lax.broadcasted_iota(jnp.int32, shape, 0)
    query_id = lax.broadcasted_iota(jnp.int32, shape, 1)
    key_column = lax.broadcasted_iota(jnp.int32, (size, 1), 0)
    query_row = lax.broadcasted_iota(jnp.int32, (1, size), 1)
    together = segment_of(key_column, lengths_ref) == segment_of(query_row, lengths_ref)
    seen = together & ((columns_ref[:, 3:4] > 0) | (key_id == query_id))
    same_ref[...] = (columns_ref[:, 2:3] == rows_ref[2:3, :]).astype(jnp.float32)
    hidden_ref[...] = jnp.where(seen, 0.0, masked_score)


def turn(values, cosine, sine):
    width = values.shape[1]
    lane = lax.broadcasted_iota(jnp.int32, values.shape, 1)
    other = jnp.where(
        lane % 64 < 32, pltpu.roll(values, width - 32, 1), pltpu.roll(values, 32, 1)
    )
    return values * cosine + other * sine


def head_lanes(values, head):
    lane = lax.broadcasted_iota(jnp.int32, values.shape, 1)
    return jnp.where((lane < 64) == (head == 0), values, jnp.zeros_like(values))


def project(input_ref, weight_refs, cosine_ref, sine_ref, out_ref, scale):
    width = weight_refs[0].shape[0]
    cosine = jnp.concatenate([cosine_ref[...]] * 2, axis=1)
    sine = jnp.concatenate([sine_ref[...]] * 2, axis=1)

    def one(i, carry):
        def columns(part):
            return pl.ds(pl.multiple_of(part * width + i * 256, 256), 256)

        at = pl.ds(pl.multiple_of(i * 256, 256), 256)
        query = matmul(input_ref[...], weight_refs[0][:, at])
        out_ref[:, columns(0)] = (turn(query, cosine, sine) * scale).astype(jnp.bfloat16)
        key = matmul(input_ref[...], weight_refs[1][:, at])
        out_ref[:, columns(1)] = turn(key, cosine, sine).astype(jnp.bfloat16)
        out_ref[:, columns(2)] = matmul(input_ref[...], weight_refs[2][:, at]).astype(
            jnp.bfloat16
        )
        return carry

    lax.fori_loop(0, width // 256, one, 0)


def attend_pair(pair, width, heads_ref, bias_ref, same_ref, hidden_ref, out_ref, log_ref):
    def columns(part):
        return pl.ds(pl.multiple_of(part * width + pair * 128, 128), 128)

    query, key, value = (heads_ref[:, columns(part)] for part in range(3))
    total = None
    for which in (0, 1):
        head = 2 * pair + which
        gap = bias_ref[0, head] - bias_ref[1, head]
        scores = matmul(head_lanes(key, which), query, 1, 1)
        scores = scores + same_ref[...] * gap + hidden_ref[...]
        top = jnp.max(scores, axis=0, keepdims=True)
        weights = jnp.exp(scores - top)
        weight_sum = jnp.sum(weights, axis=0, keepdims=True)
        log_ref[pl.ds(head, 1), :] = top + jnp.log(weight_sum)
        soft = (weights * (1.0 / weight_sum)).astype(jnp.bfloat16)
        part = matmul(head_lanes(value, which), soft, 0, 0)
        total = part if total is None else total + part
    out_ref[:, pl.ds(pl.multiple_of(pair * 128, 128), 128)] = total.T.astype(jnp.bfloat16)


def normed(values):
    factor = lax.rsqrt(jnp.mean(values * values, axis=-1, keepdims=True) + epsilon)
    return values * factor, factor


def forward_body(refs, between, loaded):
    (
        arrived_ref, columns_ref, rows_ref, lengths_ref, bias_ref, gain_ref,
        query_w_ref, key_w_ref, value_w_ref, cosine_ref, sine_ref,
        stream_ref, input_ref, heads_ref, out_ref, log_ref,
        same_ref, hidden_ref,
    ) = refs
    width = gain_ref.shape[1]
    scale = 1.0 / math.sqrt(64)
    pair_masks(columns_ref, rows_ref, lengths_ref, same_ref, hidden_ref)
    chosen = pick_rows(columns_ref[:, 1:2], arrived_ref.shape[0])
    loaded(0)
    matmul_columns(stream_ref, chosen, arrived_ref)
    stream = stream_ref[...].astype(jnp.float32)
    input_ref[...] = (normed(stream)[0] * gain_ref[...]).astype(jnp.bfloat16)
    weight_refs = (query_w_ref, key_w_ref, value_w_ref)
    for i in (1, 2, 3):
        loaded(i)
    project(input_ref, weight_refs, cosine_ref, sine_ref, heads_ref, scale)

    def one(pair, carry):
        between(pair)
        attend_pair(pair, width, heads_ref, bias_ref, same_ref, hidden_ref, out_ref, log_ref)
        return carry

    lax.fori_loop(0, width // 128, one, 0)


def fold_lanes(row):
    folded = row[:, 0:128]
    for i in range(1, row.shape[1] // 128):
        folded += row[:, i * 128 : (i + 1) * 128]
    return folded


def square_into(stats_ref, at, values, columns_ref):
    valid = (columns_ref[:, 3:4] > 0).astype(jnp.float32)
    across = jnp.sum(values * values * valid, axis=0, keepdims=True)
    stats_ref[at : at + 1, :] = fold_lanes(across)


def attend_back_pair(
    pair, width, scale, heads_ref, do_ref, bias_ref, log_ref, same_ref, hidden_ref, cosine_ref,
    sine_ref, grads_ref, bias_same_ref, bias_all_ref,
):
    half = jnp.bfloat16

    def columns(part):
        return pl.ds(pl.multiple_of(part * width + pair * 128, 128), 128)

    query, key, value = (heads_ref[:, columns(part)] for part in range(3))
    grad_out = do_ref[:, columns(0)]
    query_t = key_grad = value_grad = None
    for which in (0, 1):
        head = 2 * pair + which
        gap = bias_ref[0, head] - bias_ref[1, head]
        key_part = head_lanes(key, which)
        scores = matmul(key_part, query, 1, 1)
        scores = scores + same_ref[...] * gap + hidden_ref[...]
        soft = jnp.exp(scores - log_ref[pl.ds(head, 1), :])
        grad_soft = matmul(head_lanes(value, which), grad_out, 1, 1)
        inner = jnp.sum(soft * grad_soft, axis=0, keepdims=True)
        grad_scores = (soft * (grad_soft - inner)).astype(half)
        wide = grad_scores.astype(jnp.float32)
        bias_all_ref[pl.ds(head, 1), :] = jnp.sum(wide, axis=0, keepdims=True)
        bias_same_ref[pl.ds(head, 1), :] = jnp.sum(wide * same_ref[...], axis=0, keepdims=True)
        parts = (
            matmul(key_part, grad_scores, 0, 0),
            matmul(grad_scores, head_lanes(query, which)),
            matmul(soft.astype(half), head_lanes(grad_out, which)),
        )
        if which == 0:
            query_t, key_grad, value_grad = parts
        else:
            query_t, key_grad, value_grad = (
                query_t + parts[0],
                key_grad + parts[1],
                value_grad + parts[2],
            )
    cosine, sine = cosine_ref[...], -sine_ref[...]
    grads_ref[:, columns(0)] = (turn(query_t.T, cosine, sine) * scale).astype(half)
    grads_ref[:, columns(1)] = turn(key_grad, cosine, sine).astype(half)
    grads_ref[:, columns(2)] = value_grad.astype(half)


def feed_forward(refs, weights, gates_out, ups_out, hidden_out, scratch, saves, between):
    columns_ref, rows_ref, gain_ref, stream_ref, attended_ref, out_w_ref = refs[:6]
    packed_ref, middle_ref, input_ref, stats_ref = refs[6:]
    (
        gate_buf, up_buf, down_buf, gates_buf, ups_buf, hidden_buf, mlp_ref,
        load_sems, store_sems,
    ) = scratch
    tile = gate_buf.shape[2]
    tiles = gates_out.shape[1] // tile
    half = jnp.bfloat16

    def at(i):
        return pl.ds(pl.multiple_of(i * tile, tile), tile)

    def loads(i):
        slot = lax.rem(i, 2)
        return [
            pltpu.make_async_copy(weights[0].at[:, at(i)], gate_buf.at[slot], load_sems.at[slot, 0]),
            pltpu.make_async_copy(weights[1].at[:, at(i)], up_buf.at[slot], load_sems.at[slot, 1]),
            pltpu.make_async_copy(weights[2].at[at(i)], down_buf.at[slot], load_sems.at[slot, 2]),
        ]

    def stores(i):
        slot = lax.rem(i, 2)
        return [
            pltpu.make_async_copy(gates_buf.at[slot], gates_out.at[:, at(i)], store_sems.at[slot, 0]),
            pltpu.make_async_copy(ups_buf.at[slot], ups_out.at[:, at(i)], store_sems.at[slot, 1]),
            pltpu.make_async_copy(
                hidden_buf.at[slot], hidden_out.at[:, at(i)], store_sems.at[slot, 2]
            ),
        ]

    for copy in loads(0):
        copy.start()
    stats_ref[...] = jnp.zeros_like(stats_ref)
    stream = stream_ref[...].astype(jnp.float32)
    square_into(stats_ref, 0, stream, columns_ref)
    matmul_columns(mlp_ref, attended_ref[...], out_w_ref)
    attn_out = mlp_ref[...]
    square_into(stats_ref, 1, attn_out, columns_ref)
    middle = stream + attn_out
    square_into(stats_ref, 2, middle, columns_ref)
    middle_ref[...] = middle
    input_ref[...] = (normed(middle)[0] * gain_ref[...]).astype(half)
    for copy in saves:
        copy.start()
    mlp_ref[...] = jnp.zeros_like(mlp_ref)

    def one(i, carry):
        slot = lax.rem(i, 2)
        between(i)
        for copy in loads(i):
            copy.wait()

        @pl.when(i + 1 < tiles)
        def _():
            for copy in loads(i + 1):
                copy.start()

        @pl.when(i >= 2)
        def _():
            for copy in stores(i - 2):
                copy.wait()

        gate = matmul(input_ref[...], gate_buf[slot])
        up = matmul(input_ref[...], up_buf[slot])
        gates_buf[slot] = gate
        ups_buf[slot] = up
        hidden = (gate * jax.nn.sigmoid(gate) * up).astype(half)
        hidden_buf[slot] = hidden
        for copy in stores(i):
            copy.start()
        mlp_ref[...] += matmul(hidden, down_buf[slot])
        return carry

    lax.fori_loop(0, tiles, one, 0)
    valid = (columns_ref[:, 3:4] > 0).astype(jnp.float32)
    mlp_out = mlp_ref[...]
    result = middle_ref[...] + mlp_out
    placed = place_rows(rows_ref[1:2, :], packed_ref.shape[0])
    mlp_ref[...] = result
    matmul_columns(packed_ref, placed, mlp_ref)
    square_into(stats_ref, 3, mlp_out, columns_ref)
    square_into(stats_ref, 4, result, columns_ref)
    lane = lax.broadcasted_iota(jnp.int32, (valid.shape[0], 128), 1)
    stats_ref[5:6, :] = jnp.sum(jnp.where(lane == 0, valid, 0.0), axis=0, keepdims=True)
    for i in (tiles - 2, tiles - 1):
        for copy in stores(i):
            copy.wait()


def forward_gather_kernel(shards, lents, swap_count, compute_counts, *refs):
    ins, outs = compute_counts
    total = len(lents) + swap_count
    in_refs, refs = refs[: ins + total], refs[ins + total :]
    out_refs, refs = refs[: outs + total], refs[outs + total :]
    masks, out_w_buf, out_w_sem, feed_scratch, staged, sems, scratch = (
        refs[:2], refs[2], refs[3], refs[4:13], refs[13:24], refs[24:26], refs[26:],
    )
    work = GatherAll(
        Spot(shards), lents, swap_count, in_refs[ins:], out_refs[outs:], scratch
    )
    work.start()
    *attend_ins, gain_mlp_ref = in_refs[:ins]
    arriving, leaving = staged[:4], staged[4:]
    loads = [
        pltpu.make_async_copy(attend_ins[at], arriving[i], sems[0].at[i])
        for i, at in enumerate((0, 6, 7, 8))
    ]
    for copy in loads:
        copy.start()
    attend_ins[0], attend_ins[6:9] = arriving[0], arriving[1:4]
    attend_outs, feed_outs = leaving[:5], [*out_refs[5:9], *leaving[5:], out_refs[outs - 1]]
    saves = [
        pltpu.make_async_copy(leaving[i], out_refs[at], sems[1].at[i])
        for i, at in enumerate((0, 1, 2, 3, 4, 9, 10))
    ]
    pairs = attend_ins[5].shape[1] // 128

    tiles = out_refs[5].shape[1] // feed_scratch[0].shape[2]

    def between(pair):
        work.exchange(pair, pairs + tiles)
        work.steps(pair, pairs)

    forward_body(
        (*attend_ins, *attend_outs, *masks), between, lambda i: loads[i].wait()
    )
    for copy in saves[:5]:
        copy.start()
    work.finish_gathers()
    full_refs = out_refs[outs:]
    copy = pltpu.make_async_copy(full_refs[0], out_w_buf, out_w_sem)
    copy.start()
    copy.wait()
    gates_out, ups_out, hidden_out, *feed_outs = feed_outs
    feed_forward(
        (
            attend_ins[1], attend_ins[2], gain_mlp_ref, attend_outs[0], attend_outs[3], out_w_buf,
            *feed_outs,
        ),
        full_refs[1:4], gates_out, ups_out, hidden_out, feed_scratch, saves[5:],
        lambda i: work.exchange(pairs + i, pairs + tiles),
    )
    for copy in saves:
        copy.wait()
    for swap in work.swaps:
        swap.finish()


def forward_gather_call(
    shards, inputs, spaces, out_shape, out_specs, pieces, lents, sent, collective_id
):
    anywhere = pl.BlockSpec(memory_space=pl.ANY)
    tokens, width = out_shape[0].shape
    tile = 512
    half, full = jnp.bfloat16, jnp.float32
    counts = (len(inputs), len(out_shape))
    comm = len(pieces) + len(sent)
    results = pl.pallas_call(
        functools.partial(forward_gather_kernel, shards, lents, len(sent), counts),
        out_shape=[*out_shape, *gather_shapes(shards, pieces, sent, [])],
        in_specs=spaces + [anywhere] * comm,
        out_specs=out_specs + [anywhere] * comm,
        scratch_shapes=[
            pltpu.VMEM((tokens, tokens), full),
            pltpu.VMEM((tokens, tokens), full),
            pltpu.VMEM((width, width), half),
            DMA,
            pltpu.VMEM((2, width, tile), half),
            pltpu.VMEM((2, width, tile), half),
            pltpu.VMEM((2, tile, width), half),
            pltpu.VMEM((2, tokens, tile), full),
            pltpu.VMEM((2, tokens, tile), full),
            pltpu.VMEM((2, tokens, tile), half),
            pltpu.VMEM((tokens, width), full),
            DMA((2, 3)),
            DMA((2, 3)),
            *[pltpu.VMEM(inputs[at].shape, half) for at in (0, 6, 7, 8)],
            *[
                pltpu.VMEM(out_shape[at].shape, out_shape[at].dtype)
                for at in (0, 1, 2, 3, 4, 9, 10)
            ],
            DMA((4,)),
            DMA((7,)),
            *GatherAll.scratch(shards, len(pieces), len(sent)),
        ],
        compiler_params=pltpu.CompilerParams(
            collective_id=collective_id, has_side_effects=True, vmem_limit_bytes=VMEM_LIMIT
        ),
    )(*inputs, *pieces, *sent)
    first = len(out_shape)
    second = first + len(pieces)
    return results[:first], results[first:second], results[second:]


def input_grad_kernel(shards, lent, *refs):
    (
        columns_ref, rows_ref, lengths_ref, bias_ref, gain_mlp_ref, gain_attn_ref, middle_ref,
        out_w_ref, arrived_ref, heads_ref, log_ref, cosine_ref, sine_ref, stream_ref,
        query_w_ref, key_w_ref, value_w_ref, packed_out_ref, gates_ref, ups_ref, rows_mlp_ref,
        gate_w_ref, up_w_ref, down_w_ref,
        grads_ref, packed_ref, stats_ref, grad_down_ref,
        grad_gate_ref, grad_up_ref, home_ref, partial_ref,
        gates_buf, ups_buf, gate_buf, up_buf, down_buf, grad_gate_buf, grad_up_buf,
        back_ref, dh_ref, do_ref, same_ref, hidden_ref, bias_same_ref, bias_all_ref,
        load_sems, store_sems, weight_sems, send_sems, recv_sems, own_sem,
    ) = refs[:52]
    staged, in_sems, out_sem, refs = refs[52:59], refs[59], refs[60], refs[61:]
    arriving = [
        pltpu.make_async_copy(source, buffer, in_sems.at[i])
        for i, (source, buffer) in enumerate(
            zip(
                (arrived_ref, out_w_ref, middle_ref, heads_ref, cosine_ref, sine_ref, stream_ref),
                staged,
                strict=True,
            )
        )
    ]
    arrived_ref, out_w_ref, middle_ref, heads_ref, cosine_ref, sine_ref, stream_ref = staged
    saved_ref, grads_ref = grads_ref, refs[0]
    dy_ref, refs = refs[1], refs[2:]
    save = pltpu.make_async_copy(grads_ref, saved_ref, out_sem)
    spot = Spot(shards)
    swap = Swap(spot, packed_out_ref, home_ref, (send_sems, recv_sems), own_sem)
    reduces = [
        Reduce(spot, lent, partial_ref, grad_down_ref, refs[20 * g : 20 * g + 20], g, 2)
        for g in (0, 1)
    ]
    tile = gate_buf.shape[2]
    tiles = gates_ref.shape[1] // tile
    width = gain_attn_ref.shape[1]
    half = jnp.bfloat16

    def at(i):
        return pl.ds(pl.multiple_of(i * tile, tile), tile)

    def loads(i):
        slot = lax.rem(i, 2)
        pairs = [
            (gates_ref.at[:, at(i)], gates_buf),
            (ups_ref.at[:, at(i)], ups_buf),
            (gate_w_ref.at[:, at(i)], gate_buf),
            (up_w_ref.at[:, at(i)], up_buf),
            (down_w_ref.at[at(i)], down_buf),
        ]
        return [
            pltpu.make_async_copy(source, buffer.at[slot], load_sems.at[slot, j])
            for j, (source, buffer) in enumerate(pairs)
        ]

    def stores(i):
        slot = lax.rem(i, 2)
        pairs = [(grad_gate_buf, grad_gate_ref), (grad_up_buf, grad_up_ref)]
        return [
            pltpu.make_async_copy(buffer.at[slot], target.at[:, at(i)], store_sems.at[slot, j])
            for j, (buffer, target) in enumerate(pairs)
        ]

    def row_loads(i):
        slot = lax.rem(i, 2)
        return [
            pltpu.make_async_copy(
                rows_mlp_ref.at[:, at(i)], grad_gate_buf.at[slot], load_sems.at[slot, 0]
            )
        ]

    def row_stores(i):
        slot = lax.rem(i, 2)
        return [
            pltpu.make_async_copy(
                down_buf.at[slot], partial_ref.at[at(i)], store_sems.at[slot, 0]
            )
        ]

    pairs = width // 128
    slots = tiles + pairs
    steps = spot.half + 1

    def reduce_steps(slot):
        def one(step, carry):
            for reduce in reduces:
                reduce.step(step)
            return carry

        lax.fori_loop(slot * steps // slots, (slot + 1) * steps // slots, one, 0)

    greet(spot)
    for copy in [arriving[0], *row_loads(0), *arriving[1:]]:
        copy.start()
    chosen = pick_rows(columns_ref[:, 1:2], arrived_ref.shape[0])
    arriving[0].wait()
    matmul_columns(dy_ref, chosen, arrived_ref)

    def rows_step(i, carry):
        slot = lax.rem(i, 2)
        for copy in row_loads(i):
            copy.wait()

        @pl.when(i + 1 < tiles)
        def _():
            for copy in row_loads(i + 1):
                copy.start()

        @pl.when(i >= 2)
        def _():
            for copy in row_stores(i - 2):
                copy.wait()

        down_buf[slot] = matmul(grad_gate_buf[slot], dy_ref[...], 0, 0).astype(half)
        for copy in row_stores(i):
            copy.start()
        return carry

    lax.fori_loop(0, tiles, rows_step, 0)
    for i in (tiles - 2, tiles - 1):
        for copy in row_stores(i):
            copy.wait()
    for copy in loads(0):
        copy.start()

    def begin(item, carry):
        for reduce in reduces:
            reduce.start(item)
        return carry

    lax.fori_loop(0, spot.chips, begin, 0)
    back_ref[...] = jnp.zeros_like(back_ref)
    pair_masks(columns_ref, rows_ref, lengths_ref, same_ref, hidden_ref)
    for reduce in reduces:
        reduce.far_step(0)

    def one(i, carry):
        slot = lax.rem(i, 2)

        swap.start(i, slots)
        reduce_steps(i)
        for copy in loads(i):
            copy.wait()

        @pl.when(i + 1 < tiles)
        def _():
            for copy in loads(i + 1):
                copy.start()

        @pl.when(i >= 2)
        def _():
            for copy in stores(i - 2):
                copy.wait()

        gate, up = gates_buf[slot], ups_buf[slot]
        grad_hidden = matmul(dy_ref[...], down_buf[slot], 1, 1)
        sigmoid = jax.nn.sigmoid(gate)
        grad_gate = (grad_hidden * up * sigmoid * (1.0 + gate * (1.0 - sigmoid))).astype(half)
        grad_up = (grad_hidden * gate * sigmoid).astype(half)
        grad_gate_buf[slot] = grad_gate
        grad_up_buf[slot] = grad_up
        for copy in stores(i):
            copy.start()
        back_ref[...] += matmul(grad_gate, gate_buf[slot], 1, 1) + matmul(
            grad_up, up_buf[slot], 1, 1
        )
        return carry

    lax.fori_loop(0, tiles, one, 0)
    for copy in arriving[1:]:
        copy.wait()
    stats_ref[...] = jnp.zeros_like(stats_ref)

    def through_norm(values, grad, gain_ref, first):
        entry, factor = normed(values)
        gain_grad = jnp.sum(grad * entry, axis=0, keepdims=True)
        for i in range(width // 128):
            stats_ref[first + i : first + i + 1, :] = gain_grad[:, i * 128 : (i + 1) * 128]
        scaled = grad * gain_ref[...]
        inner = jnp.mean(scaled * entry, axis=-1, keepdims=True)
        return factor * (scaled - entry * inner)

    dh = dy_ref[...].astype(jnp.float32) + through_norm(
        middle_ref[...], back_ref[...], gain_mlp_ref, 0
    )
    dh_ref[...] = dh
    branch = dh.astype(half)
    grads_ref[:, pl.ds(3 * width, width)] = branch

    def back_out(i, carry):
        at = pl.ds(pl.multiple_of(i * 256, 256), 256)
        do_ref[:, at] = matmul(
            grads_ref[:, pl.ds(3 * width, width)], out_w_ref[at, :], 1, 1
        ).astype(half)
        return carry

    lax.fori_loop(0, width // 256, back_out, 0)
    scale = 1.0 / math.sqrt(64)
    for i in (tiles - 2, tiles - 1):
        for copy in stores(i):
            copy.wait()
    halves = [pl.ds(0, tile), pl.ds(tile, tile)]

    def weight_loads(source, buffer, which):
        return [
            pltpu.make_async_copy(source.at[:, columns], buffer.at[j], weight_sems.at[which, j])
            for j, columns in enumerate(halves)
        ]

    for copy in weight_loads(query_w_ref, gate_buf, 0) + weight_loads(key_w_ref, up_buf, 1):
        copy.start()

    def two(pair, carry):
        swap.start(tiles + pair, slots)
        reduce_steps(tiles + pair)
        attend_back_pair(
            pair, width, scale, heads_ref, do_ref, bias_ref, log_ref, same_ref, hidden_ref,
            cosine_ref, sine_ref, grads_ref, bias_same_ref, bias_all_ref,
        )
        return carry

    lax.fori_loop(0, width // 128, two, 0)
    save.start()
    heads = bias_all_ref.shape[0]
    lane = lax.broadcasted_iota(jnp.int32, (heads, 128), 1)
    row = lax.broadcasted_iota(jnp.int32, (heads, 128), 0)
    same = jnp.sum(bias_same_ref[...], axis=1, keepdims=True)
    other = jnp.sum(bias_all_ref[...], axis=1, keepdims=True) - same
    stats_ref[16:17, :] = jnp.sum(
        jnp.where(lane == row, same, 0.0) + jnp.where(lane == row + heads, other, 0.0),
        axis=0,
        keepdims=True,
    )
    def through(buffer, first):
        def one(j, carry):
            at = pl.ds(pl.multiple_of(first + j * tile, tile), tile)
            back_ref[...] += matmul(grads_ref[:, at], buffer[j], 1, 1)
            return carry

        lax.fori_loop(0, 2, one, 0)

    back_ref[...] = jnp.zeros_like(back_ref)

    for copy in weight_loads(query_w_ref, gate_buf, 0):
        copy.wait()
    through(gate_buf, 0)
    for copy in weight_loads(value_w_ref, gate_buf, 0):
        copy.start()
    for copy in weight_loads(key_w_ref, up_buf, 1):
        copy.wait()
    through(up_buf, width)
    for copy in weight_loads(value_w_ref, gate_buf, 0):
        copy.wait()
    through(gate_buf, 2 * width)
    grad_stream = dh_ref[...] + through_norm(
        stream_ref[...].astype(jnp.float32), back_ref[...], gain_attn_ref, 8
    )
    placed = place_rows(rows_ref[1:2, :], packed_ref.shape[0])
    dh_ref[...] = grad_stream
    matmul_columns(packed_ref, placed, dh_ref)
    save.wait()
    swap.finish()
    for reduce in reduces:
        reduce.finish()


def input_grad_call(shards, inputs, spaces, far_inputs, lent, collective_id):
    anywhere = pl.BlockSpec(memory_space=pl.ANY)
    inside = pl.BlockSpec(memory_space=pltpu.VMEM)
    packed, gates = far_inputs[3], far_inputs[4]
    tokens, hidden = gates.shape
    width = packed.shape[1]
    heads = inputs[10].shape[0]
    tile = 512
    assert 2 * tile == width
    half, full = jnp.bfloat16, jnp.float32
    vmem, shape = pltpu.VMEM, jax.ShapeDtypeStruct
    return pl.pallas_call(
        functools.partial(input_grad_kernel, shards, lent),
        out_shape=[
            shape((tokens, 4 * width), half),
            shape(packed.shape, half),
            shape((24, 128), full),
            Reduce.out_shape(shards, lent, shape((hidden, width), half)),
            shape((tokens, hidden), half),
            shape((tokens, hidden), half),
            shape(packed.shape, half),
            shape((hidden, width), half),
        ],
        in_specs=[*spaces, *[anywhere] * len(far_inputs)],
        out_specs=[anywhere] + [inside] * 2 + [anywhere] * 5,
        scratch_shapes=[
            vmem((2, tokens, tile), full),
            vmem((2, tokens, tile), full),
            vmem((2, width, tile), half),
            vmem((2, width, tile), half),
            vmem((2, tile, width), half),
            vmem((2, tokens, tile), half),
            vmem((2, tokens, tile), half),
            vmem((tokens, width), full),
            vmem((tokens, width), full),
            vmem((tokens, width), half),
            vmem((tokens, tokens), full),
            vmem((tokens, tokens), full),
            vmem((heads, tokens), full),
            vmem((heads, tokens), full),
            DMA((2, 5)),
            DMA((2, 2)),
            DMA((2, 2)),
            DMA((shards,)),
            DMA((shards,)),
            DMA,
            *[vmem(inputs[at].shape, inputs[at].dtype) for at in (8, 7, 6, 9, 11, 12, 13)],
            DMA((7,)),
            DMA,
            vmem((tokens, 4 * width), half),
            vmem((tokens, width), half),
            *Reduce.scratch(shards, lent, hidden // shards // 2, width) * 2,
        ],
        compiler_params=pltpu.CompilerParams(
            collective_id=collective_id, has_side_effects=True, vmem_limit_bytes=VMEM_LIMIT
        ),
    )(*inputs, *far_inputs)


def weight_grad_kernel(shards, lents, *refs):
    (
        columns_ref, input_attn_ref, attended_ref, input_mlp_ref, stats_forward_ref,
        stats_back_ref, home_out_ref, packed_ref, gate_ref, up_ref, entry_ref,
        grad_gate_ref, grad_up_ref, grad_in_ref, output_ref, input_grad_ref, sums_ref,
    ) = refs[:17]
    partials = refs[17:20]
    (
        attn_t_ref, attended_t_ref, mlp_t_ref, home_ref, stats_ref, tile_buf, part_buf,
        load_sems, store_sems, send_sems, recv_sems, own_sem,
    ) = refs[20:32]
    tally_refs, refs = refs[32:40], refs[40:]
    half, full = jnp.bfloat16, jnp.float32
    spot = Spot(shards)
    swap = Swap(spot, packed_ref, home_ref, (send_sems, recv_sems), own_sem)
    tally = Tally(spot, stats_ref, sums_ref, tally_refs)
    outputs = (grad_gate_ref, grad_up_ref, grad_in_ref)
    reduces = [
        Reduce(spot, lents[g], partials[g], outputs[g], refs[20 * g : 20 * g + 20])
        for g in range(3)
    ]
    steps = spot.half + 1
    parts = 5
    tile = tile_buf.shape[2]
    tiles = gate_ref.shape[1] // tile

    def at(i):
        return pl.ds(pl.multiple_of(i * tile, tile), tile)

    def product(source, lefts, partial, reduce):
        def load(i):
            slot = lax.rem(i, 2)
            return pltpu.make_async_copy(
                source.at[:, at(i)], tile_buf.at[slot], load_sems.at[slot]
            )

        def store(i):
            slot = lax.rem(i, 2)
            return pltpu.make_async_copy(
                part_buf.at[slot], partial.at[:, at(i)], store_sems.at[slot]
            )

        load(0).start()
        first = 0
        for left, count in lefts:

            def one(i, carry, left=left):
                slot = lax.rem(i, 2)
                load(i).wait()

                @pl.when(i + 1 < tiles)
                def _():
                    load(i + 1).start()

                @pl.when(i >= 2)
                def _():
                    store(i - 2).wait()

                part_buf[slot] = matmul(left[...], tile_buf[slot]).astype(half)
                store(i).start()
                return carry

            lax.fori_loop(first, first + count, one, 0)
            first += count
        for i in (tiles - 2, tiles - 1):
            store(i).wait()

        def begin(item, carry):
            reduce.start(item)
            return carry

        lax.fori_loop(0, spot.chips, begin, 0)
        reduce.far_step(0)

    greet(spot)
    swap.start(0, parts)
    stats_ref[0:8, :] = stats_forward_ref[...]
    stats_ref[8:32, :] = stats_back_ref[...]
    tally.start()
    mlp_t_ref[...] = input_mlp_ref[...].astype(full).T.astype(half)
    product(gate_ref, [(mlp_t_ref, tiles)], partials[0], reduces[0])
    swap.start(1, parts)
    product(up_ref, [(mlp_t_ref, tiles)], partials[1], reduces[1])
    swap.start(2, parts)
    chosen = pick_rows(columns_ref[:, 0:1], home_ref.shape[0])

    def ticks(tick, carry):
        @pl.when(tick < steps)
        def _():
            reduces[0].step(tick)

        @pl.when(tick < 2)
        def _():
            swap.start(3 + tick, parts)

        @pl.when(tick == 0)
        def _():
            attn_t_ref[...] = input_attn_ref[...].astype(full).T.astype(half)
            attended_t_ref[...] = attended_ref[...].astype(full).T.astype(half)
            product(
                entry_ref,
                [(attn_t_ref, tiles - tiles // 4), (attended_t_ref, tiles // 4)],
                partials[2],
                reduces[2],
            )

        @pl.when((tick > 0) & (tick < steps + 1))
        def _():
            reduces[1].step(tick - 1)

        @pl.when(tick == 1)
        def _():
            matmul_columns(output_ref, chosen, home_out_ref)
            tally.middle()

        @pl.when(tick > 1)
        def _():
            reduces[2].step(tick - 2)

        return carry

    lax.fori_loop(0, steps + 2, ticks, 0)
    swap.finish()
    matmul_columns(input_grad_ref, chosen, home_ref)
    tally.finish()
    for reduce in reduces:
        reduce.finish()


def weight_grad_call(shards, inputs, far_inputs, lents, collective_id):
    tile = 512
    packed, hidden = far_inputs[0], far_inputs[1].shape[1]
    tokens, width = inputs[1].shape
    assert hidden == 4 * width
    half, full = jnp.bfloat16, jnp.float32
    shape = jax.ShapeDtypeStruct
    anywhere = pl.BlockSpec(memory_space=pl.ANY)
    inside = pl.BlockSpec(memory_space=pltpu.VMEM)
    scratch = []
    for lent in lents:
        scratch += Reduce.scratch(shards, lent, width // shards, hidden)
    results = pl.pallas_call(
        functools.partial(weight_grad_kernel, shards, lents),
        out_shape=[
            *[Reduce.out_shape(shards, lent, shape((width, hidden), half)) for lent in lents],
            shape((tokens, width), half),
            shape((tokens, width), half),
            shape((32, 128), full),
            *[shape((width, hidden), half)] * 3,
        ],
        in_specs=[inside] * len(inputs) + [anywhere] * len(far_inputs),
        out_specs=[anywhere] * 3 + [inside] * 3 + [anywhere] * 3,
        scratch_shapes=[
            *[pltpu.VMEM((width, tokens), half)] * 3,
            pltpu.VMEM(packed.shape, half),
            pltpu.VMEM((32, 128), full),
            pltpu.VMEM((2, tokens, tile), half),
            pltpu.VMEM((2, width, tile), half),
            DMA((2,)),
            DMA((2,)),
            DMA((shards,)),
            DMA((shards,)),
            DMA,
            *Tally.scratch(shards, (32, 128)),
            *scratch,
        ],
        compiler_params=pltpu.CompilerParams(
            collective_id=collective_id, has_side_effects=True, vmem_limit_bytes=VMEM_LIMIT
        ),
    )(*inputs, *far_inputs)
    return results[:6]


def on_device(
    tokens,
    cotangent,
    send_slot,
    recv_slot,
    lengths,
    variate,
    valid_mask,
    norm_attn,
    w_query,
    w_key,
    w_value,
    w_out,
    variate_bias,
    norm_mlp,
    w_gate,
    w_up,
    w_down,
):
    shards = lax.axis_size("shard")
    tok_rows, width = tokens.shape
    slot_total = 2 * tok_rows
    heads = variate_bias.shape[1]
    half, full = jnp.bfloat16, jnp.float32
    share = width // shards
    indices = jnp.stack([send_slot, recv_slot, variate, valid_mask])
    rows = jnp.concatenate([indices, jnp.zeros_like(indices)])
    columns = rows.T
    _, position = layout(lengths[0], tok_rows)
    cosine, sine = angle_tables(position, width // heads)
    cosine = jnp.concatenate([cosine] * 4, axis=1)
    sine = jnp.concatenate([-sine, sine] * 2, axis=1)
    gains = jnp.stack([norm_attn, norm_mlp]).astype(full)
    gains = jnp.pad(gains, ((0, 6), (0, 128 - share)))
    shape = jax.ShapeDtypeStruct
    packed_shape = shape((slot_total, width), half)
    token_shape = shape((tok_rows, width), half)
    full_in, arrived_tokens, gains, out_cotangent = gather_call(
        shards, rows, tokens, cotangent, [w_query, w_key, w_value], (4, 4, 4), gains, 1
    )
    gains = gains.reshape(shards, 8, 128)
    gain_attn = gains[:, 0, :share].reshape(1, width)
    gain_mlp = gains[:, 1, :share].reshape(1, width)
    inside = pl.BlockSpec(memory_space=pltpu.VMEM)
    anywhere = pl.BlockSpec(memory_space=pl.ANY)
    scalar = pl.BlockSpec(memory_space=pltpu.SMEM)
    hidden = w_gate.shape[1]
    (
        (
            stream, input_attn, head_rows, attended, logs,
            gates, ups, hidden_rows, packed, middle, input_mlp, stats_forward,
        ),
        (full_out, full_gate, full_up, full_down),
        (arrived_grads,),
    ) = forward_gather_call(
        shards,
        [
            arrived_tokens, columns, rows, lengths, variate_bias, gain_attn, *full_in,
            cosine, sine, gain_mlp,
        ],
        [anywhere] + [inside] * 2 + [scalar] * 2 + [inside] + [anywhere] * 3 + [inside] * 3,
        [
            token_shape,
            token_shape,
            shape((tok_rows, 3 * width), half),
            token_shape,
            shape((heads, tok_rows), full),
            shape((tok_rows, hidden), full),
            shape((tok_rows, hidden), full),
            shape((tok_rows, hidden), half),
            packed_shape,
            shape((tok_rows, width), full),
            token_shape,
            shape((8, 128), full),
        ],
        [anywhere] * 8 + [inside] + [anywhere] * 2 + [inside],
        [w_out, w_gate, w_up, w_down],
        (2, 4, 2, 2),
        [out_cotangent],
        2,
    )
    (
        entry_grads, packed_grad, stats_back, grad_down, grad_gates, grad_ups, home_out, _,
    ) = input_grad_call(
        shards,
        [
            columns, rows, lengths, variate_bias, gain_mlp, gain_attn, middle, full_out,
            arrived_grads, head_rows, logs, cosine, sine, stream,
        ],
        [inside] * 2
        + [scalar] * 2
        + [inside] * 2
        + [anywhere] * 4
        + [inside]
        + [anywhere] * 3,
        [*full_in, packed, gates, ups, hidden_rows, full_gate, full_up, full_down],
        4,
        3,
    )
    grad_gate, grad_up, grad_in, output, input_grad, sums = weight_grad_call(
        shards,
        [columns, input_attn, attended, input_mlp, stats_forward, stats_back, home_out],
        [packed_grad, grad_gates, grad_ups, entry_grads],
        (4, 2, 2),
        4,
    )
    rep = lax.axis_index("rep").astype(jnp.int32).reshape(1, 1)
    (
        output, input_grad, grad_gate, grad_up, grad_down,
        grad_query, grad_key, grad_value, grad_out,
    ) = local_call(
        assemble_kernel,
        [
            token_shape,
            token_shape,
            *[shape((share, hidden), full)] * 2,
            shape((hidden // shards, width), full),
            *[shape((share, width), full)] * 4,
        ],
        [rep, grad_gate, grad_up, grad_down, grad_in, output, input_grad],
        [scalar] + [inside] * 6,
        [pltpu.VMEM((share, hidden), full)],
    )
    squares = jnp.sum(sums[0:6], axis=1)
    root_means = jnp.sqrt(squares[:5] / (squares[5] * width))
    share_start = lax.axis_index("shard") * share
    grad_norm_mlp = lax.dynamic_slice_in_dim(sums[8:16].reshape(-1), share_start, share)
    grad_norm_attn = lax.dynamic_slice_in_dim(sums[16:24].reshape(-1), share_start, share)
    bias_grads = sums[24, : 2 * heads].reshape(2, heads)
    return (
        output,
        input_grad,
        grad_norm_attn,
        grad_query,
        grad_key,
        grad_value,
        grad_out,
        bias_grads,
        grad_norm_mlp,
        grad_gate,
        grad_up,
        grad_down,
        root_means,
    )


def solution(mesh):
    in_specs = (
        P(("rep", "shard"), None),
        P(("rep", "shard"), None),
        P(("rep", "shard")),
        P(("rep", "shard")),
        P(("rep", "shard"), None),
        P(("rep", "shard")),
        P(("rep", "shard")),
        P("shard"),
        P("shard", None),
        P("shard", None),
        P("shard", None),
        P("shard", None),
        P(),
        P("shard"),
        P("shard", None),
        P("shard", None),
        P("shard", None),
    )
    out_specs = (
        P(("rep", "shard"), None),
        P(("rep", "shard"), None),
        P("shard"),
        P("shard", None),
        P("shard", None),
        P("shard", None),
        P("shard", None),
        P(),
        P("shard"),
        P("shard", None),
        P("shard", None),
        P("shard", None),
        P(),
    )
    return jax.shard_map(
        on_device, mesh=mesh, in_specs=in_specs, out_specs=out_specs, check_vma=False
    )
```

profile of v0, /device:TPU:8, one launch (start us, length us, event | category | flops | bytes accessed | tf_op | source)
XLA Modules:
  0.0 494.9 jit_solution(2983821373097360975)
XLA Ops:
  0.6 0.8 reduce-window.4
  1.5 0.1 convert_reduce_fusion
  1.6 0.7 fusion.8
  2.2 0.1 select_reduce_fusion
  2.3 1.0 fusion
  3.3 1.3 pad_maximum_fusion
  4.6 1.4 concatenate.9.refs_0_.refs_2_.refs_1_
  5.9 1.3 fusion.7.refs_6_
  7.2 72.6 %shard_map.264 = (bf16[1024,1024]{1,0:T(8,128)(2,1)}, bf16[1024,1024]{1,0:T(8,128)(2,1)}, bf16[1024,1024]{1,0:T(8,128)(2,1)}, bf16[1024,1024]{1,0:T(8,128)(2,1)}...) custom-call(s32[8,512]{1,0:T(8,128)} %concatenate.9.refs_0_.refs_2_.refs_1_, bf16[512,1024]{1,0:T(8,128)(2,1)} %refs_1_.1, ...), custom_call_target="tpu_custom_call" | custom-call | tf_op jit(solution)/shard_map/pallas_call | solution.py:378
  79.8 0.9 fusion.9
  80.8 0.7 reshape_squeeze.10.refs_11_.refs_4_
  81.4 0.7 reshape_squeeze.9.refs_5_
  82.1 1.6 copy.50
  83.7 148.3 %shard_map.265 = (bf16[512,1024]{1,0:T(8,128)(2,1)}, bf16[512,1024]{1,0:T(8,128)(2,1)}, bf16[512,3072]{1,0:T(8,128)(2,1)}, bf16[512,1024]{1,0:T(8,128)(2,1)}, f3...) custom-call(bf16[1024,1024]{1,0:T(8,128)(2,1)} %get-tuple-element.58, ...), custom_call_target="tpu_custom_call" | custom-call | tf_op jit(solution)/shard_map/pallas_call | solution.py:1095
  232.0 99.5 %shard_map.266 = (bf16[512,4096]{1,0:T(8,128)(2,1)}, bf16[1024,1024]{1,0:T(8,128)(2,1)}, f32[24,128]{1,0:T(8,128)}, bf16[2,256,512]{2,1,0:T(8,128)(2,1)}, bf16[5...) custom-call(s32[512,8]{1,0:T(8,128)} %bitcast.29, ...), custom_call_target="tpu_custom_call" | custom-call | tf_op jit(solution)/shard_map/pallas_call | solution.py:1409
  331.5 153.5 %shard_map.267 = (bf16[2,64,2048]{2,1,0:T(8,128)(2,1)}, bf16[2,64,3072]{2,1,0:T(8,128)(2,1)}, bf16[2,64,3072]{2,1,0:T(8,128)(2,1)}, bf16[512,1024]{1,0:T(8,128)(...) custom-call(s32[512,8]{1,0:T(8,128)} %bitcast.30, ...), custom_call_target="tpu_custom_call" | custom-call | tf_op jit(solution)/shard_map/pallas_call | solution.py:1598
  485.0 0.9 slice_reduce_fusion
  485.8 0.6 slice.31
  487.1 0.5 divide_sqrt_fusion
  487.6 5.4 %shard_map.268 = (bf16[512,1024]{1,0:T(8,128)(2,1)}, bf16[512,1024]{1,0:T(8,128)(2,1)}, f32[64,4096]{1,0:T(8,128)}, f32[64,4096]{1,0:T(8,128)}, f32[256,1024]{1,...) custom-call(s32[1,1]{1,0:T(1,128)} %bitcast.rep_ref, ...), custom_call_target="tpu_custom_call" | custom-call | tf_op jit(solution)/shard_map/pallas_call | solution.py:755
  493.1 0.0 copy-done
  493.1 0.6 dynamic_slice.6
  493.7 0.6 dynamic_slice.7
  494.3 0.6 reshape_squeeze.11
  (6 shorter events, 0.0 us)
Async XLA Ops:
  485.0 8.1 %copy-start = (f32[32,128]{1,0:T(8,128)S(1)}, f32[32,128]{1,0:T(8,128)}, u32[]{:S(2)}) copy-start(f32[32,128]{1,0:T(8,128)} %get-tuple-element.95) | copy-start | bytes 49156
where the time goes:
time: 497 us; the launch traced here: 495 us
  Pallas kernels  479 us (96%)
  local copies, waits for them, and re-layouts  7.6 us (2%)
  other arithmetic  6.6 us (1%)
    pallas_call x1, Pallas kernels, weight_grad_call(): pl.pallas_call(functools.partial(weight_grad_kernel, shards, lents), out_...  153 us
    pallas_call x1, Pallas kernels, forward_gather_call(): pl.pallas_call(functools.partial(forward_gather_kernel, shards, lents, le...  148 us
    pallas_call x1, Pallas kernels, input_grad_call(): pl.pallas_call(functools.partial(input_grad_kernel, shards, lent), out_sh...  99.5 us
    pallas_call x1, Pallas kernels, gather_call(): pl.pallas_call(functools.partial(gather_kernel, shards, lents), out_shape...  72.6 us

commit v1 on v0

--- a/solution.py
+++ b/solution.py
@@ -3,6 +3,7 @@
 
 import jax
 import jax.numpy as jnp
+import numpy as np
 from jax import lax
 from jax.experimental import pallas as pl
 from jax.experimental.pallas import tpu as pltpu
@@ -13,23 +14,6 @@
 epsilon = 1e-06
 masked_score = -1e30
 VMEM_LIMIT = 62 << 20
-
-
-def angle_tables(position, head_dim):
-    half_dim = head_dim // 2
-    inverse_freq = 1.0 / 10000.0 ** (jnp.arange(half_dim, dtype=jnp.float32) / half_dim)
-    theta_angle = position.astype(jnp.float32)[:, None] * inverse_freq[None, :]
-    return (jnp.cos(theta_angle), jnp.sin(theta_angle))
-
-
-def layout(lengths_row, tok_rows):
-    slot_ids = jnp.arange(tok_rows, dtype=jnp.int32)
-    seq_ends = jnp.cumsum(lengths_row)
-    segment = jnp.sum((slot_ids[:, None] >= seq_ends[None, :]).astype(jnp.int32), axis=1)
-    starts = seq_ends - lengths_row
-    chosen = segment[:, None] == jnp.arange(lengths_row.shape[0], dtype=jnp.int32)[None, :]
-    begins = jnp.sum(jnp.where(chosen, starts[None, :], 0), axis=1)
-    return (segment, slot_ids - begins)
 
 
 def ring_place(chip, chips):
@@ -332,12 +316,15 @@
 
 def gather_kernel(shards, lents, *refs):
     spot = Spot(shards)
-    rows_ref, tokens_ref, cotangent_ref = refs[:3]
+    rows_ref, tokens_ref, cotangent_ref, lengths_ref, frequency_ref = refs[:5]
     count = len(lents)
-    pieces, gains_ref, refs = refs[3 : 3 + count], refs[3 + count], refs[4 + count :]
-    outputs, packed_out, refs = refs[: count + 2], refs[count + 2], refs[count + 3 :]
-    packed_ref, scratch = refs[0], refs[1:]
-    work = GatherAll(spot, lents, 2, [*pieces, packed_ref, gains_ref], outputs, scratch)
+    pieces, gains_ref, refs = refs[5 : 5 + count], refs[5 + count], refs[6 + count :]
+    outputs, packed_out, refs = refs[: count + 1], refs[count + 1], refs[count + 2 :]
+    cosine_ref, sine_ref, columns_ref, *gain_refs = refs[:5]
+    packed_ref, all_gains_ref, scratch = refs[5], refs[6], refs[7:]
+    work = GatherAll(
+        spot, lents, 2, [*pieces, packed_ref, gains_ref], [*outputs, all_gains_ref], scratch
+    )
     work.start()
     chosen = place_rows(rows_ref[0:1, :], packed_ref.shape[0])
     matmul_columns(packed_ref, chosen, tokens_ref)
@@ -348,12 +335,17 @@
         @pl.when(hop == 0)
         def _():
             matmul_columns(packed_out, chosen, cotangent_ref)
+            angle_tables(lengths_ref, frequency_ref, cosine_ref, sine_ref)
+            columns_ref[...] = rows_ref[...].T
 
         work.steps(hop, spot.half)
         return carry
 
     lax.fori_loop(0, spot.half, one, 0)
     work.finish()
+    share = tokens_ref.shape[1] // shards
+    for gain_ref, row in zip(gain_refs, gain_rows(all_gains_ref, share), strict=True):
+        gain_ref[...] = row
 
 
 def gather_shapes(shards, pieces, sent, shared):
@@ -370,25 +362,39 @@
     )
 
 
-def gather_call(shards, rows, tokens, cotangent, pieces, lents, gains, collective_id):
+def gather_call(
+    shards, rows, tokens, cotangent, lengths, frequency, pieces, lents, gains, collective_id
+):
     anywhere = pl.BlockSpec(memory_space=pl.ANY)
     inside = pl.BlockSpec(memory_space=pltpu.VMEM)
     count = len(pieces)
     packed = jax.ShapeDtypeStruct((2 * tokens.shape[0], tokens.shape[1]), tokens.dtype)
     results = pl.pallas_call(
         functools.partial(gather_kernel, shards, lents),
-        out_shape=[*gather_shapes(shards, pieces, [packed], [gains]), packed],
-        in_specs=[inside] * 3 + [anywhere] * (count + 1),
-        out_specs=[anywhere] * (count + 2) + [inside],
+        out_shape=[
+            *gather_shapes(shards, pieces, [packed], []),
+            packed,
+            *[jax.ShapeDtypeStruct((tokens.shape[0], 128), jnp.float32)] * 2,
+            jax.ShapeDtypeStruct(rows.shape[::-1], rows.dtype),
+            *[jax.ShapeDtypeStruct((1, tokens.shape[1]), jnp.float32)] * 2,
+        ],
+        in_specs=[
+            *[inside] * 3,
+            pl.BlockSpec(memory_space=pltpu.SMEM),
+            inside,
+            *[anywhere] * (count + 1),
+        ],
+        out_specs=[anywhere] * (count + 1) + [inside] * 6,
         scratch_shapes=[
             pltpu.VMEM(packed.shape, packed.dtype),
+            pltpu.VMEM((8 * shards, 128), jnp.float32),
             *GatherAll.scratch(shards, count, 2),
         ],
         compiler_params=pltpu.CompilerParams(
             collective_id=collective_id, has_side_effects=True, vmem_limit_bytes=VMEM_LIMIT
         ),
-    )(rows, tokens, cotangent, *pieces, gains)
-    return results[:count], *results[count:]
+    )(rows, tokens, cotangent, lengths, frequency, *pieces, gains)
+    return results
 
 
 class Reduce:
@@ -771,6 +777,37 @@
         + (index >= second).astype(jnp.int32)
         + (index >= third).astype(jnp.int32)
     )
+
+
+def angle_tables(lengths_ref, frequency_ref, cosine_ref, sine_ref):
+    index = lax.broadcasted_iota(jnp.int32, (cosine_ref.shape[0], 1), 0)
+    segment = segment_of(index, lengths_ref)
+    begin = jnp.zeros_like(index)
+    end = 0
+    for i in range(3):
+        end = end + lengths_ref[0, i]
+        begin = jnp.where(segment == i + 1, end, begin)
+    angle = (index - begin).astype(jnp.float32) * frequency_ref[...]
+    lane = lax.broadcasted_iota(jnp.int32, angle.shape, 1)
+    sine = jnp.sin(angle)
+    cosine_ref[...] = jnp.cos(angle)
+    sine_ref[...] = jnp.where(lane % 64 < 32, -sine, sine)
+
+
+def gain_rows(gains_ref, share):
+    shards = gains_ref.shape[0] // 8
+    rows = []
+    for which in (0, 1):
+        parts = []
+        for first in range(0, shards * share, 128):
+            total = jnp.zeros((1, 128), jnp.float32)
+            for lane in range(0, 128, share):
+                at = (first + lane) // share * 8 + which
+                part = gains_ref[at : at + 1, :]
+                total += part if lane == 0 else pltpu.roll(part, lane, 1)
+            parts.append(total)
+        rows.append(jnp.concatenate(parts, axis=1))
+    return rows
 
 
 def pair_masks(columns_ref, rows_ref, lengths_ref, same_ref, hidden_ref):
@@ -1541,9 +1578,8 @@
     chosen = pick_rows(columns_ref[:, 0:1], home_ref.shape[0])
 
     def ticks(tick, carry):
-        @pl.when(tick < steps)
-        def _():
-            reduces[0].step(tick)
+        reduces[0].step(tick)
+        reduces[1].step(tick)
 
         @pl.when(tick < 2)
         def _():
@@ -1560,22 +1596,16 @@
                 reduces[2],
             )
 
-        @pl.when((tick > 0) & (tick < steps + 1))
-        def _():
-            reduces[1].step(tick - 1)
-
         @pl.when(tick == 1)
         def _():
             matmul_columns(output_ref, chosen, home_out_ref)
             tally.middle()
 
-        @pl.when(tick > 1)
-        def _():
-            reduces[2].step(tick - 2)
+        reduces[2].step(tick)
 
         return carry
 
-    lax.fori_loop(0, steps + 2, ticks, 0)
+    lax.fori_loop(0, steps, ticks, 0)
     swap.finish()
     matmul_columns(input_grad_ref, chosen, home_ref)
     tally.finish()
@@ -1654,22 +1684,20 @@
     share = width // shards
     indices = jnp.stack([send_slot, recv_slot, variate, valid_mask])
     rows = jnp.concatenate([indices, jnp.zeros_like(indices)])
-    columns = rows.T
-    _, position = layout(lengths[0], tok_rows)
-    cosine, sine = angle_tables(position, width // heads)
-    cosine = jnp.concatenate([cosine] * 4, axis=1)
-    sine = jnp.concatenate([-sine, sine] * 2, axis=1)
+    pair_count = width // heads // 2
+    frequency = 1.0 / 10000.0 ** (np.arange(pair_count, dtype=np.float32) / pair_count)
+    frequency = jnp.asarray(np.tile(frequency, 128 // pair_count)[None], full)
     gains = jnp.stack([norm_attn, norm_mlp]).astype(full)
     gains = jnp.pad(gains, ((0, 6), (0, 128 - share)))
     shape = jax.ShapeDtypeStruct
     packed_shape = shape((slot_total, width), half)
     token_shape = shape((tok_rows, width), half)
-    full_in, arrived_tokens, gains, out_cotangent = gather_call(
-        shards, rows, tokens, cotangent, [w_query, w_key, w_value], (4, 4, 4), gains, 1
-    )
-    gains = gains.reshape(shards, 8, 128)
-    gain_attn = gains[:, 0, :share].reshape(1, width)
-    gain_mlp = gains[:, 1, :share].reshape(1, width)
+    *full_in, arrived_tokens, out_cotangent, cosine, sine, columns, gain_attn, gain_mlp = (
+        gather_call(
+            shards, rows, tokens, cotangent, lengths, frequency, [w_query, w_key, w_value],
+            (4, 4, 4), gains, 1,
+        )
+    )
     inside = pl.BlockSpec(memory_space=pltpu.VMEM)
     anywhere = pl.BlockSpec(memory_space=pl.ANY)
     scalar = pl.BlockSpec(memory_space=pltpu.SMEM)

time: 497 us -> 487 us (0.980)
  no operation moved by 1% of the time
where the time goes in v1:
time: 487 us; the launch traced here: 485 us
  Pallas kernels  478 us (98%)
    pallas_call x1, Pallas kernels, weight_grad_call(): pl.pallas_call(functools.partial(weight_grad_kernel, shards, lents), out_...  151 us
    pallas_call x1, Pallas kernels, forward_gather_call(): pl.pallas_call(functools.partial(forward_gather_kernel, shards, lents, le...  148 us
    pallas_call x1, Pallas kernels, input_grad_call(): pl.pallas_call(functools.partial(input_grad_kernel, shards, lent), out_sh...  99.6 us
    pallas_call x1, Pallas kernels, gather_call(): pl.pallas_call(functools.partial(gather_kernel, shards, lents), out_shape...  73 us

profile of v1, /device:TPU:8, one launch (start us, length us, event | category | flops | bytes accessed | tf_op | source)
XLA Modules:
  0.0 485.3 jit_solution(7785623067908091795)
XLA Ops:
  0.7 1.4 concatenate.3.refs_0_.refs_2_.refs_1_
  2.0 1.3 fusion.6.refs_8_
  3.3 73.0 %shard_map.273 = (bf16[1024,1024]{1,0:T(8,128)(2,1)}, bf16[1024,1024]{1,0:T(8,128)(2,1)}, bf16[1024,1024]{1,0:T(8,128)(2,1)}, bf16[1024,1024]{1,0:T(8,128)(2,1)}...) custom-call(s32[8,512]{1,0:T(8,128)} %concatenate.3.refs_0_.refs_2_., ...), custom_call_target="tpu_custom_call" | custom-call | tf_op jit(solution)/shard_map/pallas_call | solution.py:372
  76.3 148.2 %shard_map.274 = (bf16[512,1024]{1,0:T(8,128)(2,1)}, bf16[512,1024]{1,0:T(8,128)(2,1)}, bf16[512,3072]{1,0:T(8,128)(2,1)}, bf16[512,1024]{1,0:T(8,128)(2,1)}, f3...) custom-call(bf16[1024,1024]{1,0:T(8,128)(2,1)} %get-tuple-element.63, ...), custom_call_target="tpu_custom_call" | custom-call | tf_op jit(solution)/shard_map/pallas_call | solution.py:1132
  224.6 99.6 %shard_map.275 = (bf16[512,4096]{1,0:T(8,128)(2,1)}, bf16[1024,1024]{1,0:T(8,128)(2,1)}, f32[24,128]{1,0:T(8,128)}, bf16[2,256,512]{2,1,0:T(8,128)(2,1)}, bf16[5...) custom-call(s32[512,8]{1,0:T(8,128)} %get-tuple-element.62.refs_1_.ref, ...), custom_call_target="tpu_custom_call" | custom-call | tf_op jit(solution)/shard_map/pallas_call | solution.py:1446
  324.1 151.3 %shard_map.276 = (bf16[2,64,2048]{2,1,0:T(8,128)(2,1)}, bf16[2,64,3072]{2,1,0:T(8,128)(2,1)}, bf16[2,64,3072]{2,1,0:T(8,128)(2,1)}, bf16[512,1024]{1,0:T(8,128)(...) custom-call(s32[512,8]{1,0:T(8,128)} %get-tuple-element.62.refs_1_.r, ...), custom_call_target="tpu_custom_call" | custom-call | tf_op jit(solution)/shard_map/pallas_call | solution.py:1628
  475.4 0.0 copy-start
  475.4 0.9 slice_reduce_fusion
  476.3 0.6 slice.23
  477.5 0.5 divide_sqrt_fusion
  478.0 5.4 %shard_map.277 = (bf16[512,1024]{1,0:T(8,128)(2,1)}, bf16[512,1024]{1,0:T(8,128)(2,1)}, f32[64,4096]{1,0:T(8,128)}, f32[64,4096]{1,0:T(8,128)}, f32[256,1024]{1,...) custom-call(s32[1,1]{1,0:T(1,128)} %bitcast.rep_ref, ...), custom_call_target="tpu_custom_call" | custom-call | tf_op jit(solution)/shard_map/pallas_call | solution.py:761
  483.5 0.0 copy-done
  483.5 0.6 dynamic_slice.6
  484.1 0.6 dynamic_slice.7
  484.7 0.6 reshape_squeeze.3
  (3 shorter events, 0.0 us)
Async XLA Ops:
  475.4 8.1 %copy-start = (f32[32,128]{1,0:T(8,128)S(1)}, f32[32,128]{1,0:T(8,128)}, u32[]{:S(2)}) copy-start(f32[32,128]{1,0:T(8,128)} %get-tuple-element.103) | copy-start | bytes 49156

commit v2 on v1

--- a/solution.py
+++ b/solution.py
@@ -725,8 +725,13 @@
 
 
 def assemble_kernel(rep_ref, *refs):
-    raws, plain, refs = refs[:4], refs[4:6], refs[6:]
-    plain_outs, outs, whole_ref = refs[:2], refs[2:9], refs[9]
+    raws, plain, sums_ref, refs = refs[:4], refs[4:6], refs[6], refs[7:]
+    plain_outs, outs, root_ref, whole_ref = refs[:2], refs[2:9], refs[9], refs[10]
+    square = jnp.sum(sums_ref[0:8, :], axis=1, keepdims=True)
+    root = jnp.sqrt(square / (square[5:6, :] * plain_outs[0].shape[1]))
+    row = lax.broadcasted_iota(jnp.int32, (8, 128), 0)
+    lane = lax.broadcasted_iota(jnp.int32, (8, 128), 1)
+    root_ref[...] = jnp.sum(jnp.where(row == lane, root, 0.0), axis=0, keepdims=True)
     for source, target in zip(plain, plain_outs, strict=True):
         target[...] = source[...]
     for raw_ref, out_ref in zip(raws, [*outs[:3], whole_ref], strict=True):
@@ -756,16 +761,29 @@
         outs[3 + i][...] = whole_ref[:, i * width : (i + 1) * width]
 
 
-def local_call(kernel, out_shape, inputs, spaces=None, scratch=()):
-    inside = pl.BlockSpec(memory_space=pltpu.VMEM)
+def assemble_call(rep, raws, plain, sums, shapes):
+    def halves(array):
+        *lead, rows, columns = array.shape
+        return pl.BlockSpec(
+            (*lead, rows // 2, columns), lambda i: (0,) * len(lead) + (i, 0)
+        )
+
+    root = jax.ShapeDtypeStruct((1, 128), jnp.float32)
+    inputs = [*raws, *plain]
+    largest = raws[-1]
+    columns = sum(each.shape[1] for each in shapes[-4:])
     return pl.pallas_call(
-        kernel,
-        out_shape=out_shape,
-        in_specs=spaces or [inside] * len(inputs),
-        out_specs=[inside] * len(out_shape),
-        scratch_shapes=list(scratch),
+        assemble_kernel,
+        out_shape=[*shapes, root],
+        grid=(2,),
+        in_specs=[pl.BlockSpec(memory_space=pltpu.SMEM)]
+        + [halves(each) for each in inputs]
+        + [pl.BlockSpec(sums.shape, lambda i: (0, 0))],
+        out_specs=[halves(each) for each in shapes]
+        + [pl.BlockSpec(root.shape, lambda i: (0, 0))],
+        scratch_shapes=[pltpu.VMEM((largest.shape[1] // 2, columns), jnp.float32)],
         compiler_params=pltpu.CompilerParams(vmem_limit_bytes=VMEM_LIMIT),
-    )(*inputs)
+    )(rep, *inputs, sums)
 
 
 def segment_of(index, lengths_ref):
@@ -1502,7 +1520,14 @@
         attn_t_ref, attended_t_ref, mlp_t_ref, home_ref, stats_ref, tile_buf, part_buf,
         load_sems, store_sems, send_sems, recv_sems, own_sem,
     ) = refs[20:32]
-    tally_refs, refs = refs[32:40], refs[40:]
+    tally_refs, staged, in_sems, refs = refs[32:40], refs[40:44], refs[44], refs[45:]
+    arriving = [
+        pltpu.make_async_copy(source, buffer, in_sems.at[i])
+        for i, (source, buffer) in enumerate(
+            zip((input_mlp_ref, input_attn_ref, attended_ref, home_out_ref), staged, strict=True)
+        )
+    ]
+    input_mlp_ref, input_attn_ref, attended_ref, home_out_ref = staged
     half, full = jnp.bfloat16, jnp.float32
     spot = Spot(shards)
     swap = Swap(spot, packed_ref, home_ref, (send_sems, recv_sems), own_sem)
@@ -1567,9 +1592,12 @@
 
     greet(spot)
     swap.start(0, parts)
+    for copy in arriving:
+        copy.start()
     stats_ref[0:8, :] = stats_forward_ref[...]
     stats_ref[8:32, :] = stats_back_ref[...]
     tally.start()
+    arriving[0].wait()
     mlp_t_ref[...] = input_mlp_ref[...].astype(full).T.astype(half)
     product(gate_ref, [(mlp_t_ref, tiles)], partials[0], reduces[0])
     swap.start(1, parts)
@@ -1587,6 +1615,8 @@
 
         @pl.when(tick == 0)
         def _():
+            for copy in arriving[1:]:
+                copy.wait()
             attn_t_ref[...] = input_attn_ref[...].astype(full).T.astype(half)
             attended_t_ref[...] = attended_ref[...].astype(full).T.astype(half)
             product(
@@ -1634,7 +1664,11 @@
             shape((32, 128), full),
             *[shape((width, hidden), half)] * 3,
         ],
-        in_specs=[inside] * len(inputs) + [anywhere] * len(far_inputs),
+        in_specs=[inside]
+        + [anywhere] * 3
+        + [inside] * 2
+        + [anywhere]
+        + [anywhere] * len(far_inputs),
         out_specs=[anywhere] * 3 + [inside] * 3 + [anywhere] * 3,
         scratch_shapes=[
             *[pltpu.VMEM((width, tokens), half)] * 3,
@@ -1648,6 +1682,8 @@
             DMA((shards,)),
             DMA,
             *Tally.scratch(shards, (32, 128)),
+            *[pltpu.VMEM(inputs[at].shape, half) for at in (3, 1, 2, 6)],
+            DMA((4,)),
             *scratch,
         ],
         compiler_params=pltpu.CompilerParams(
@@ -1732,7 +1768,7 @@
         ],
         [anywhere] * 8 + [inside] + [anywhere] * 2 + [inside],
         [w_out, w_gate, w_up, w_down],
-        (2, 4, 2, 2),
+        (4, 4, 2, 2),
         [out_cotangent],
         2,
     )
@@ -1764,9 +1800,12 @@
     rep = lax.axis_index("rep").astype(jnp.int32).reshape(1, 1)
     (
         output, input_grad, grad_gate, grad_up, grad_down,
-        grad_query, grad_key, grad_value, grad_out,
-    ) = local_call(
-        assemble_kernel,
+        grad_query, grad_key, grad_value, grad_out, root_means,
+    ) = assemble_call(
+        rep,
+        [grad_gate, grad_up, grad_down, grad_in],
+        [output, input_grad],
+        sums,
         [
             token_shape,
             token_shape,
@@ -1774,12 +1813,8 @@
             shape((hidden // shards, width), full),
             *[shape((share, width), full)] * 4,
         ],
-        [rep, grad_gate, grad_up, grad_down, grad_in, output, input_grad],
-        [scalar] + [inside] * 6,
-        [pltpu.VMEM((share, hidden), full)],
-    )
-    squares = jnp.sum(sums[0:6], axis=1)
-    root_means = jnp.sqrt(squares[:5] / (squares[5] * width))
+    )
+    root_means = root_means[0, :5]
     share_start = lax.axis_index("shard") * share
     grad_norm_mlp = lax.dynamic_slice_in_dim(sums[8:16].reshape(-1), share_start, share)
     grad_norm_attn = lax.dynamic_slice_in_dim(sums[16:24].reshape(-1), share_start, share)

time: 487 us -> 480 us (0.986)
  Pallas kernels: 478 us -> 472 us
where the time goes in v2:
time: 480 us; the launch traced here: 478 us
  Pallas kernels  472 us (98%)
    pallas_call x1, Pallas kernels, weight_grad_call(): pl.pallas_call(functools.partial(weight_grad_kernel, shards, lents), out_...  148 us
    pallas_call x1, Pallas kernels, forward_gather_call(): pl.pallas_call(functools.partial(forward_gather_kernel, shards, lents, le...  146 us
    pallas_call x1, Pallas kernels, input_grad_call(): pl.pallas_call(functools.partial(input_grad_kernel, shards, lent), out_sh...  99.6 us
    pallas_call x1, Pallas kernels, gather_call(): pl.pallas_call(functools.partial(gather_kernel, shards, lents), out_shape...  73.1 us

profile of v2, /device:TPU:8, one launch (start us, length us, event | category | flops | bytes accessed | tf_op | source)
XLA Modules:
  0.0 478.3 jit_solution(6288182070810560776)
XLA Ops:
  0.7 1.4 concatenate.3.refs_0_.refs_2_.refs_1_
  2.0 1.3 fusion.6.refs_8_
  3.3 73.1 %shard_map.273 = (bf16[1024,1024]{1,0:T(8,128)(2,1)}, bf16[1024,1024]{1,0:T(8,128)(2,1)}, bf16[1024,1024]{1,0:T(8,128)(2,1)}, bf16[1024,1024]{1,0:T(8,128)(2,1)}...) custom-call(s32[8,512]{1,0:T(8,128)} %concatenate.3.refs_0_.refs_2_., ...), custom_call_target="tpu_custom_call" | custom-call | tf_op jit(solution)/shard_map/pallas_call | solution.py:372
  76.4 145.8 %shard_map.274 = (bf16[512,1024]{1,0:T(8,128)(2,1)}, bf16[512,1024]{1,0:T(8,128)(2,1)}, bf16[512,3072]{1,0:T(8,128)(2,1)}, bf16[512,1024]{1,0:T(8,128)(2,1)}, f3...) custom-call(bf16[1024,1024]{1,0:T(8,128)(2,1)} %get-tuple-element.64, ...), custom_call_target="tpu_custom_call" | custom-call | tf_op jit(solution)/shard_map/pallas_call | solution.py:1150
  222.2 99.6 %shard_map.275 = (bf16[512,4096]{1,0:T(8,128)(2,1)}, bf16[1024,1024]{1,0:T(8,128)(2,1)}, f32[24,128]{1,0:T(8,128)}, bf16[2,256,512]{2,1,0:T(8,128)(2,1)}, bf16[5...) custom-call(s32[512,8]{1,0:T(8,128)} %get-tuple-element.63.refs_1_.ref, ...), custom_call_target="tpu_custom_call" | custom-call | tf_op jit(solution)/shard_map/pallas_call | solution.py:1464
  321.7 148.4 %shard_map.276 = (bf16[2,64,2048]{2,1,0:T(8,128)(2,1)}, bf16[2,64,3072]{2,1,0:T(8,128)(2,1)}, bf16[2,64,3072]{2,1,0:T(8,128)(2,1)}, bf16[512,1024]{1,0:T(8,128)(...) custom-call(s32[512,8]{1,0:T(8,128)} %get-tuple-element.63.refs_1_.r, ...), custom_call_target="tpu_custom_call" | custom-call | tf_op jit(solution)/shard_map/pallas_call | solution.py:1658
  470.2 0.0 copy-start
  470.2 5.1 %shard_map.277 = (bf16[512,1024]{1,0:T(8,128)(2,1)}, bf16[512,1024]{1,0:T(8,128)(2,1)}, f32[64,4096]{1,0:T(8,128)}, f32[64,4096]{1,0:T(8,128)}, f32[256,1024]{1,...) custom-call(s32[1,1]{1,0:T(1,128)} %bitcast.rep_ref, ...), custom_call_target="tpu_custom_call" | custom-call | tf_op jit(solution)/shard_map/pallas_call | solution.py:775
  475.3 1.2 slice_bitcast_fusion.2
  476.4 0.0 copy-done
  476.4 0.6 dynamic_slice.6
  477.0 0.6 dynamic_slice.7
  477.6 0.6 reshape_squeeze.3
  (3 shorter events, 0.0 us)
Async XLA Ops:
  470.2 6.2 %copy-start = (f32[32,128]{1,0:T(8,128)S(1)}, f32[32,128]{1,0:T(8,128)}, u32[]{:S(2)}) copy-start(f32[32,128]{1,0:T(8,128)} %get-tuple-element.102.refs_6_) | copy-start | bytes 49156

commit v3 on v2

--- a/solution.py
+++ b/solution.py
@@ -1278,6 +1278,9 @@
     greet(spot)
     for copy in [arriving[0], *row_loads(0), *arriving[1:]]:
         copy.start()
+    early = slots // 4
+    for slot in range(early):
+        swap.start(slot, slots)
     chosen = pick_rows(columns_ref[:, 1:2], arrived_ref.shape[0])
     arriving[0].wait()
     matmul_columns(dy_ref, chosen, arrived_ref)
@@ -1323,7 +1326,7 @@
     def one(i, carry):
         slot = lax.rem(i, 2)
 
-        swap.start(i, slots)
+        swap.start(early + i, slots)
         reduce_steps(i)
         for copy in loads(i):
             copy.wait()
@@ -1397,7 +1400,7 @@
         copy.start()
 
     def two(pair, carry):
-        swap.start(tiles + pair, slots)
+        swap.start(early + tiles + pair, slots)
         reduce_steps(tiles + pair)
         attend_back_pair(
             pair, width, scale, heads_ref, do_ref, bias_ref, log_ref, same_ref, hidden_ref,

time: 480 us -> 473 us (0.985)
  Pallas kernels: 472 us -> 466 us
    pallas_call x1, Pallas kernels: 99.6 us -> 93.6 us  [input_grad_call(): pl.pallas_call(functools.partial(input_grad_kernel, shards, lent), out_sh...]
where the time goes in v3:
time: 473 us; the launch traced here: 472 us
  Pallas kernels  466 us (99%)
    pallas_call x1, Pallas kernels, weight_grad_call(): pl.pallas_call(functools.partial(weight_grad_kernel, shards, lents), out_...  148 us
    pallas_call x1, Pallas kernels, forward_gather_call(): pl.pallas_call(functools.partial(forward_gather_kernel, shards, lents, le...  146 us
    pallas_call x1, Pallas kernels, input_grad_call(): pl.pallas_call(functools.partial(input_grad_kernel, shards, lent), out_sh...  93.6 us
    pallas_call x1, Pallas kernels, gather_call(): pl.pallas_call(functools.partial(gather_kernel, shards, lents), out_shape...  73.1 us

profile of v3, /device:TPU:8, one launch (start us, length us, event | category | flops | bytes accessed | tf_op | source)
XLA Modules:
  0.0 472.1 jit_solution(9565453303199068269)
XLA Ops:
  0.7 1.4 concatenate.3.refs_0_.refs_2_.refs_1_
  2.0 1.3 fusion.6.refs_8_
  3.3 73.1 %shard_map.273 = (bf16[1024,1024]{1,0:T(8,128)(2,1)}, bf16[1024,1024]{1,0:T(8,128)(2,1)}, bf16[1024,1024]{1,0:T(8,128)(2,1)}, bf16[1024,1024]{1,0:T(8,128)(2,1)}...) custom-call(s32[8,512]{1,0:T(8,128)} %concatenate.3.refs_0_.refs_2_., ...), custom_call_target="tpu_custom_call" | custom-call | tf_op jit(solution)/shard_map/pallas_call | solution.py:372
  76.4 145.8 %shard_map.274 = (bf16[512,1024]{1,0:T(8,128)(2,1)}, bf16[512,1024]{1,0:T(8,128)(2,1)}, bf16[512,3072]{1,0:T(8,128)(2,1)}, bf16[512,1024]{1,0:T(8,128)(2,1)}, f3...) custom-call(bf16[1024,1024]{1,0:T(8,128)(2,1)} %get-tuple-element.64, ...), custom_call_target="tpu_custom_call" | custom-call | tf_op jit(solution)/shard_map/pallas_call | solution.py:1150
  222.2 93.6 %shard_map.275 = (bf16[512,4096]{1,0:T(8,128)(2,1)}, bf16[1024,1024]{1,0:T(8,128)(2,1)}, f32[24,128]{1,0:T(8,128)}, bf16[2,256,512]{2,1,0:T(8,128)(2,1)}, bf16[5...) custom-call(s32[512,8]{1,0:T(8,128)} %get-tuple-element.63.refs_1_.ref, ...), custom_call_target="tpu_custom_call" | custom-call | tf_op jit(solution)/shard_map/pallas_call | solution.py:1467
  315.7 148.3 %shard_map.276 = (bf16[2,64,2048]{2,1,0:T(8,128)(2,1)}, bf16[2,64,3072]{2,1,0:T(8,128)(2,1)}, bf16[2,64,3072]{2,1,0:T(8,128)(2,1)}, bf16[512,1024]{1,0:T(8,128)(...) custom-call(s32[512,8]{1,0:T(8,128)} %get-tuple-element.63.refs_1_.r, ...), custom_call_target="tpu_custom_call" | custom-call | tf_op jit(solution)/shard_map/pallas_call | solution.py:1661
  464.0 0.0 copy-start
  464.0 5.1 %shard_map.277 = (bf16[512,1024]{1,0:T(8,128)(2,1)}, bf16[512,1024]{1,0:T(8,128)(2,1)}, f32[64,4096]{1,0:T(8,128)}, f32[64,4096]{1,0:T(8,128)}, f32[256,1024]{1,...) custom-call(s32[1,1]{1,0:T(1,128)} %bitcast.rep_ref, ...), custom_call_target="tpu_custom_call" | custom-call | tf_op jit(solution)/shard_map/pallas_call | solution.py:775
  469.1 1.2 slice_bitcast_fusion.2
  470.2 0.0 copy-done
  470.2 0.6 dynamic_slice.6
  470.8 0.6 dynamic_slice.7
  471.4 0.6 reshape_squeeze.3
  (3 shorter events, 0.0 us)
Async XLA Ops:
  464.0 6.2 %copy-start = (f32[32,128]{1,0:T(8,128)S(1)}, f32[32,128]{1,0:T(8,128)}, u32[]{:S(2)}) copy-start(f32[32,128]{1,0:T(8,128)} %get-tuple-element.102.refs_6_) | copy-start | bytes 49156
